TPU v7x, 32 devices: a whole 2x2x4 slice. The times are simulated.
32 devices in a mesh: fsdp: 4 (over y, core), ctx: 4 (over z), tp: 2 (over x).
Axes of the slice: x: 2, y: 2, z: 4, core: 2. Of those that a mesh axis runs over, the one named last changes fastest.
Arguments:
- tokens: bfloat16 [2, 4, 1056, 1536], P(None, 'fsdp', 'ctx'), may hold values from -6 to 6
- conditioning: bfloat16 [2, 4, 130, 768], P(None, 'fsdp'), may hold values from -6 to 6
- cotangent: bfloat16 [2, 4, 1056, 1536], P(None, 'fsdp', 'ctx'), may hold values from -6 to 6
- live: int32 [2, 4], P(None, 'fsdp'), may hold values from 0 to 1, as said below
- gain_attn: bfloat16 [1536], P('fsdp'), may hold values from 0.5 to 1.5
- w_query: bfloat16 [1536, 1536], P('fsdp', 'tp'), may hold values from -0.15625 to 0.15625
- w_key: bfloat16 [1536, 1536], P('fsdp', 'tp'), may hold values from -0.15625 to 0.15625
- w_value: bfloat16 [1536, 1536], P('fsdp', 'tp'), may hold values from -0.15625 to 0.15625
- w_out: bfloat16 [1536, 1536], P('tp', 'fsdp'), may hold values from -0.625 to 0.625
- gain_cross: bfloat16 [1536], P('fsdp'), may hold values from 0.5 to 1.5
- w_cquery: bfloat16 [1536, 1536], P('fsdp', 'tp'), may hold values from -0.15625 to 0.15625
- w_ckey: bfloat16 [768, 1536], P('fsdp', 'tp'), may hold values from -0.21875 to 0.21875
- w_cvalue: bfloat16 [768, 1536], P('fsdp', 'tp'), may hold values from -0.21875 to 0.21875
- w_cout: bfloat16 [1536, 1536], P('tp', 'fsdp'), may hold values from -0.4375 to 0.4375
- gain_mlp: bfloat16 [1536], P('fsdp'), may hold values from 0.5 to 1.5
- w_gate: bfloat16 [1536, 6144], P('fsdp', 'tp'), may hold values from -0.15625 to 0.15625
- w_up: bfloat16 [1536, 6144], P('fsdp', 'tp'), may hold values from -0.15625 to 0.15625
- w_down: bfloat16 [6144, 1536], P('tp', 'fsdp'), may hold values from -0.078125 to 0.078125
Outputs:
- output: bfloat16 [2, 4, 1056, 1536], P(None, 'fsdp', 'ctx')
- grad_tokens: bfloat16 [2, 4, 1056, 1536], P(None, 'fsdp', 'ctx')
- grad_gain_attn: float32 [1536], P('fsdp')
- grad_query: float32 [1536, 1536], P('fsdp', 'tp')
- grad_key: float32 [1536, 1536], P('fsdp', 'tp')
- grad_value: float32 [1536, 1536], P('fsdp', 'tp')
- grad_out: float32 [1536, 1536], P('tp', 'fsdp')
- grad_gain_cross: float32 [1536], P('fsdp')
- grad_cquery: float32 [1536, 1536], P('fsdp', 'tp')
- grad_ckey: float32 [768, 1536], P('fsdp', 'tp')
- grad_cvalue: float32 [768, 1536], P('fsdp', 'tp')
- grad_cout: float32 [1536, 1536], P('tp', 'fsdp')
- grad_gain_mlp: float32 [1536], P('fsdp')
- grad_gate: float32 [1536, 6144], P('fsdp', 'tp')
- grad_up: float32 [1536, 6144], P('fsdp', 'tp')
- grad_down: float32 [6144, 1536], P('tp', 'fsdp')
Inputs may be any that keep to these rules, and one draw needn't show every extreme that they name: Micro-batches before the last have every slot live; the last has exactly 3 live slots.
All inputs are finite; a program needn't handle non-finite values.
Results may differ from a plain program's by a relative error of at most 0.024.
Values may be sent and summed in bfloat16 or wider, within the bound.
A program may use at most 320 MiB of HBM per device.

v0:
```python
import jax
import jax.numpy as jnp
from jax import lax
from jax.sharding import PartitionSpec as P

HD = 64
ROT = 32
LEN = 1025


HIGH = lax.Precision.HIGHEST
F32 = jnp.float32
B16 = jnp.bfloat16


def fetch_forward(ws):
    return (
        lax.all_gather(ws[0], "fsdp", axis=0, tiled=True),
        lax.all_gather(ws[1], "fsdp", axis=0, tiled=True),
        lax.all_gather(ws[2], "fsdp", axis=0, tiled=True),
        lax.all_gather(ws[3], "fsdp", axis=0, tiled=True),
        lax.all_gather(ws[4], "fsdp", axis=1, tiled=True),
        lax.all_gather(ws[5], "fsdp", axis=0, tiled=True),
        lax.all_gather(ws[6], "fsdp", axis=0, tiled=True),
        lax.all_gather(ws[7], "fsdp", axis=0, tiled=True),
        lax.all_gather(ws[8], "fsdp", axis=0, tiled=True),
        lax.all_gather(ws[9], "fsdp", axis=1, tiled=True),
        lax.all_gather(ws[10], "fsdp", axis=0, tiled=True),
        lax.all_gather(ws[11], "fsdp", axis=0, tiled=True),
        lax.all_gather(ws[12], "fsdp", axis=0, tiled=True),
        lax.all_gather(ws[13], "fsdp", axis=1, tiled=True),
    )


def fetch_backward(ws):
    return (
        lax.all_gather(ws[0], "fsdp", axis=0, tiled=True),
        lax.all_gather(ws[1], "fsdp", axis=0, tiled=True),
        lax.all_gather(ws[2], "fsdp", axis=0, tiled=True),
        lax.all_gather(ws[3], "fsdp", axis=0, tiled=True),
        lax.all_gather(ws[4], "fsdp", axis=1, tiled=True),
        lax.all_gather(ws[5], "fsdp", axis=0, tiled=True),
        lax.all_gather(ws[6], "fsdp", axis=0, tiled=True),
        lax.all_gather(ws[7], "fsdp", axis=0, tiled=True),
        lax.all_gather(ws[8], "fsdp", axis=0, tiled=True),
        lax.all_gather(ws[9], "fsdp", axis=1, tiled=True),
        lax.all_gather(ws[10], "fsdp", axis=0, tiled=True),
        lax.all_gather(ws[11], "fsdp", axis=0, tiled=True),
        lax.all_gather(ws[12], "fsdp", axis=0, tiled=True),
        lax.all_gather(ws[13], "fsdp", axis=1, tiled=True),
    )


def reduce_grads(gs):
    shares = (
        lax.psum_scatter(
            gs[0].astype(jnp.bfloat16), "fsdp", scatter_dimension=0, tiled=True
        ).astype(jnp.float32),
        lax.psum_scatter(
            gs[1].astype(jnp.bfloat16), "fsdp", scatter_dimension=0, tiled=True
        ).astype(jnp.float32),
        lax.psum_scatter(
            gs[2].astype(jnp.bfloat16), "fsdp", scatter_dimension=0, tiled=True
        ).astype(jnp.float32),
        lax.psum_scatter(
            gs[3].astype(jnp.bfloat16), "fsdp", scatter_dimension=0, tiled=True
        ).astype(jnp.float32),
        lax.psum_scatter(
            gs[4].astype(jnp.bfloat16), "fsdp", scatter_dimension=1, tiled=True
        ).astype(jnp.float32),
        lax.psum_scatter(
            gs[5].astype(jnp.bfloat16), "fsdp", scatter_dimension=0, tiled=True
        ).astype(jnp.float32),
        lax.psum_scatter(
            gs[6].astype(jnp.bfloat16), "fsdp", scatter_dimension=0, tiled=True
        ).astype(jnp.float32),
        lax.psum_scatter(
            gs[7].astype(jnp.bfloat16), "fsdp", scatter_dimension=0, tiled=True
        ).astype(jnp.float32),
        lax.psum_scatter(
            gs[8].astype(jnp.bfloat16), "fsdp", scatter_dimension=0, tiled=True
        ).astype(jnp.float32),
        lax.psum_scatter(
            gs[9].astype(jnp.bfloat16), "fsdp", scatter_dimension=1, tiled=True
        ).astype(jnp.float32),
        lax.psum_scatter(
            gs[10].astype(jnp.bfloat16), "fsdp", scatter_dimension=0, tiled=True
        ).astype(jnp.float32),
        lax.psum_scatter(
            gs[11].astype(jnp.bfloat16), "fsdp", scatter_dimension=0, tiled=True
        ).astype(jnp.float32),
        lax.psum_scatter(
            gs[12].astype(jnp.bfloat16), "fsdp", scatter_dimension=0, tiled=True
        ).astype(jnp.float32),
        lax.psum_scatter(
            gs[13].astype(jnp.bfloat16), "fsdp", scatter_dimension=1, tiled=True
        ).astype(jnp.float32),
    )
    return (
        lax.psum(shares[0].astype(jnp.bfloat16), "ctx").astype(jnp.float32),
        lax.psum(shares[1].astype(jnp.bfloat16), "ctx").astype(jnp.float32),
        lax.psum(shares[2].astype(jnp.bfloat16), "ctx").astype(jnp.float32),
        lax.psum(shares[3].astype(jnp.bfloat16), "ctx").astype(jnp.float32),
        lax.psum(shares[4].astype(jnp.bfloat16), "ctx").astype(jnp.float32),
        lax.psum(shares[5].astype(jnp.bfloat16), "ctx").astype(jnp.float32),
        lax.psum(shares[6].astype(jnp.bfloat16), "ctx").astype(jnp.float32),
        lax.psum(shares[7].astype(jnp.bfloat16), "ctx").astype(jnp.float32),
        lax.psum(shares[8].astype(jnp.bfloat16), "ctx").astype(jnp.float32),
        lax.psum(shares[9].astype(jnp.bfloat16), "ctx").astype(jnp.float32),
        lax.psum(shares[10].astype(jnp.bfloat16), "ctx").astype(jnp.float32),
        lax.psum(shares[11].astype(jnp.bfloat16), "ctx").astype(jnp.float32),
        lax.psum(shares[12].astype(jnp.bfloat16), "ctx").astype(jnp.float32),
        lax.psum(shares[13].astype(jnp.bfloat16), "ctx").astype(jnp.float32),
    )


def branch_sum(value):
    return lax.psum(value, "tp")


def input_sum(value):
    return lax.psum(value, "tp")


def normalize(value):
    feature_average = jnp.mean(value, -1, keepdims=True)
    cent = value - feature_average
    inverse_deviation = lax.rsqrt(jnp.mean(cent * cent, -1, keepdims=True) + 1e-05)
    return (cent * inverse_deviation, inverse_deviation)


def layer_norm_backward(norm_input_gradient, normalized_input, inverse_deviation, norm_gain_vector):
    gain_gradient_total = jnp.sum(norm_input_gradient * normalized_input, 0)
    normalized_gradient = norm_input_gradient * norm_gain_vector
    grad_in = inverse_deviation * (
        normalized_gradient
        - jnp.mean(normalized_gradient, -1, keepdims=True)
        - normalized_input * jnp.mean(normalized_gradient * normalized_input, -1, keepdims=True)
    )
    return (grad_in, gain_gradient_total)


def rotate(value, cosine, sine):
    half = ROT // 2
    first = value[..., :half]
    second = value[..., half:ROT]
    return jnp.concatenate(
        [first * cosine - second * sine, second * cosine + first * sine, value[..., ROT:]], axis=-1
    )


def scores_of(query, keys, scale):
    return jnp.einsum("qhd,khd->hqk", query, keys, preferred_element_type=F32) * scale


def per_device(
    tokens,
    conditioning,
    cotangent,
    live,
    gain_attn,
    w_query,
    w_key,
    w_value,
    w_out,
    gain_cross,
    w_cquery,
    w_ckey,
    w_cvalue,
    w_cout,
    gain_mlp,
    w_gate,
    w_up,
    w_down,
):
    shards = (
        gain_attn,
        w_query,
        w_key,
        w_value,
        w_out,
        gain_cross,
        w_cquery,
        w_ckey,
        w_cvalue,
        w_cout,
        gain_mlp,
        w_gate,
        w_up,
        w_down,
    )
    micro = tokens.shape[0]
    blk = tokens.shape[2]
    heads_dev = w_query.shape[1] // HD
    inner_dim = heads_dev * HD
    cond_rows = conditioning.shape[2]
    scale = HD ** (-0.5)
    ctx_count = lax.axis_size("ctx")
    ctx_here = lax.axis_index("ctx")
    base = LEN // ctx_count
    extra = LEN % ctx_count
    first_token = ctx_here * base + jnp.minimum(ctx_here, extra)
    own_count = base + (ctx_here < extra).astype(jnp.int32)
    rows_here = jnp.arange(blk, dtype=jnp.int32)
    row_ok = rows_here < own_count
    position = first_token + rows_here
    slots = jnp.arange(blk * ctx_count, dtype=jnp.int32)
    slot_block = slots // blk
    key_ok = slots % blk < base + (slot_block < extra).astype(jnp.int32)
    half = ROT // 2
    freq = 10000.0 ** (-jnp.arange(half, dtype=F32) * 2.0 / ROT)
    angle = position.astype(F32)[:, None] * freq[None, :]
    cosine = jnp.cos(angle)[:, None, :]
    sine = jnp.sin(angle)[:, None, :]
    totals = None
    outputs = []
    grad_outputs = []
    for step in range(micro):
        xf = tokens[step, 0].astype(F32)
        cond_b = conditioning[step, 0]
        keep = (row_ok & (live[step, 0] > 0)).astype(F32)[:, None]
        fw = fetch_forward(shards)
        g1 = fw[0].astype(F32)
        g2 = fw[5].astype(F32)
        g3 = fw[10].astype(F32)
        hat1, inv1 = normalize(xf)
        h1 = (hat1 * g1).astype(B16)
        query = rotate(
            jnp.dot(h1, fw[1], preferred_element_type=F32).reshape(blk, heads_dev, HD), cosine, sine
        ).astype(B16)
        keys = rotate(
            jnp.dot(h1, fw[2], preferred_element_type=F32).reshape(blk, heads_dev, HD), cosine, sine
        ).astype(B16)
        values = (
            jnp.dot(h1, fw[3], preferred_element_type=F32).astype(B16).reshape(blk, heads_dev, HD)
        )
        all_keys, all_values = (
            lax.all_gather(keys, "ctx", axis=0, tiled=True),
            lax.all_gather(values, "ctx", axis=0, tiled=True),
        )
        scores = jnp.where(key_ok[None, None, :], scores_of(query, all_keys, scale), -1e30)
        top = jnp.max(scores, -1, keepdims=True)
        expd = jnp.exp(scores - top)
        total_exp = jnp.sum(expd, -1, keepdims=True)
        log_total = top + jnp.log(total_exp)
        probs_b = (expd / total_exp).astype(B16)
        att = (
            jnp.einsum("hqk,khd->qhd", probs_b, all_values, preferred_element_type=F32)
            .reshape(blk, inner_dim)
            .astype(B16)
        )
        x1 = xf + branch_sum(jnp.dot(att, fw[4], preferred_element_type=F32))
        hat2, inv2 = normalize(x1)
        h2 = (hat2 * g2).astype(B16)
        cquery = (
            jnp.dot(h2, fw[6], preferred_element_type=F32).astype(B16).reshape(blk, heads_dev, HD)
        )
        ckeys = (
            jnp.dot(cond_b, fw[7], preferred_element_type=F32)
            .astype(B16)
            .reshape(cond_rows, heads_dev, HD)
        )
        cvalues = (
            jnp.dot(cond_b, fw[8], preferred_element_type=F32)
            .astype(B16)
            .reshape(cond_rows, heads_dev, HD)
        )
        cscores = scores_of(cquery, ckeys, scale)
        ctop = jnp.max(cscores, -1, keepdims=True)
        cexp = jnp.exp(cscores - ctop)
        cprobs = cexp / jnp.sum(cexp, -1, keepdims=True)
        cprobs_b = cprobs.astype(B16)
        catt = (
            jnp.einsum("hqk,khd->qhd", cprobs_b, cvalues, preferred_element_type=F32)
            .reshape(blk, inner_dim)
            .astype(B16)
        )
        x2 = x1 + branch_sum(jnp.dot(catt, fw[9], preferred_element_type=F32))
        hat3, inv3 = normalize(x2)
        h3 = (hat3 * g3).astype(B16)
        gate = jnp.dot(h3, fw[11], preferred_element_type=F32)
        upper = jnp.dot(h3, fw[12], preferred_element_type=F32)
        sig = jax.nn.sigmoid(gate)
        act = gate * sig
        hidden = (act * upper).astype(B16)
        result = x2 + branch_sum(jnp.dot(hidden, fw[13], preferred_element_type=F32))
        outputs.append((result * keep).astype(B16))
        bw = fetch_backward(shards)
        grad_y = cotangent[step, 0].astype(F32) * keep
        grad_yb = grad_y.astype(B16)
        grad_down = jnp.einsum("rf,rd->fd", hidden, grad_yb, preferred_element_type=F32)
        grad_hid = jnp.einsum("rd,fd->rf", grad_yb, bw[13], preferred_element_type=F32)
        grad_gate_b = (grad_hid * upper * sig * (1.0 + gate * (1.0 - sig))).astype(B16)
        grad_up_b = (grad_hid * act).astype(B16)
        grad_gate = jnp.einsum("rd,rf->df", h3, grad_gate_b, preferred_element_type=F32)
        grad_up = jnp.einsum("rd,rf->df", h3, grad_up_b, preferred_element_type=F32)
        grad_h3 = input_sum(
            jnp.einsum("rf,df->rd", grad_gate_b, bw[11], preferred_element_type=F32)
            + jnp.einsum("rf,df->rd", grad_up_b, bw[12], preferred_element_type=F32)
        )
        grad_in3, grad_g3 = layer_norm_backward(grad_h3, hat3, inv3, bw[10].astype(F32))
        grad_x2 = grad_y + grad_in3
        grad_cb = grad_x2.astype(B16)
        grad_cout = jnp.einsum("rk,rd->kd", catt, grad_cb, preferred_element_type=F32)
        grad_catt = (
            jnp.einsum("rd,kd->rk", grad_cb, bw[9], preferred_element_type=F32)
            .astype(B16)
            .reshape(blk, heads_dev, HD)
        )
        grad_cp = jnp.einsum("qhd,khd->hqk", grad_catt, cvalues, preferred_element_type=F32)
        grad_cs = (cprobs * (grad_cp - jnp.sum(cprobs * grad_cp, -1, keepdims=True))).astype(B16)
        grad_cq = (
            (jnp.einsum("hqk,khd->qhd", grad_cs, ckeys, preferred_element_type=F32) * scale)
            .reshape(blk, inner_dim)
            .astype(B16)
        )
        grad_ck = (
            jnp.einsum("hqk,qhd->khd", grad_cs, cquery, preferred_element_type=F32) * scale
        ).reshape(cond_rows, inner_dim)
        grad_cv = jnp.einsum(
            "hqk,qhd->khd", cprobs_b, grad_catt, preferred_element_type=F32
        ).reshape(cond_rows, inner_dim)
        cond_f = cond_b.astype(F32)
        grad_cquery = jnp.einsum("rd,rk->dk", h2, grad_cq, preferred_element_type=F32)
        grad_ckey = jnp.einsum("rc,rk->ck", cond_f, grad_ck, precision=HIGH)
        grad_cvalue = jnp.einsum("rc,rk->ck", cond_f, grad_cv, precision=HIGH)
        grad_h2 = input_sum(jnp.einsum("rk,dk->rd", grad_cq, bw[6], preferred_element_type=F32))
        grad_in2, grad_g2 = layer_norm_backward(grad_h2, hat2, inv2, bw[5].astype(F32))
        grad_x1 = grad_x2 + grad_in2
        grad_ab = grad_x1.astype(B16)
        grad_out = jnp.einsum("rk,rd->kd", att, grad_ab, preferred_element_type=F32)
        grad_att = (
            jnp.einsum("rd,kd->rk", grad_ab, bw[4], preferred_element_type=F32)
            .astype(B16)
            .reshape(blk, heads_dev, HD)
        )
        again = jnp.where(key_ok[None, None, :], scores_of(query, all_keys, scale), -1e30)
        probs = jnp.exp(again - log_total)
        grad_p = jnp.einsum("qhd,khd->hqk", grad_att, all_values, preferred_element_type=F32)
        grad_s = (probs * (grad_p - jnp.sum(probs * grad_p, -1, keepdims=True))).astype(B16)
        grad_q = jnp.einsum("hqk,khd->qhd", grad_s, all_keys, preferred_element_type=F32) * scale
        grad_k_all = jnp.einsum("hqk,qhd->khd", grad_s, query, preferred_element_type=F32) * scale
        grad_v_all = jnp.einsum(
            "hqk,qhd->khd", probs.astype(B16), grad_att, preferred_element_type=F32
        )
        grad_k, grad_v = (
            lax.psum_scatter(
                grad_k_all.astype(jnp.bfloat16), "ctx", scatter_dimension=0, tiled=True
            ).astype(jnp.float32),
            lax.psum_scatter(
                grad_v_all.astype(jnp.bfloat16), "ctx", scatter_dimension=0, tiled=True
            ).astype(jnp.float32),
        )
        grad_qb = rotate(grad_q, cosine, -sine).reshape(blk, inner_dim).astype(B16)
        grad_kb = rotate(grad_k, cosine, -sine).reshape(blk, inner_dim).astype(B16)
        grad_vb = grad_v.reshape(blk, inner_dim).astype(B16)
        grad_query = jnp.einsum("rd,rk->dk", h1, grad_qb, preferred_element_type=F32)
        grad_key = jnp.einsum("rd,rk->dk", h1, grad_kb, preferred_element_type=F32)
        grad_value = jnp.einsum("rd,rk->dk", h1, grad_vb, preferred_element_type=F32)
        grad_h1 = input_sum(
            jnp.einsum("rk,dk->rd", grad_qb, bw[1], preferred_element_type=F32)
            + jnp.einsum("rk,dk->rd", grad_kb, bw[2], preferred_element_type=F32)
            + jnp.einsum("rk,dk->rd", grad_vb, bw[3], preferred_element_type=F32)
        )
        grad_in1, grad_g1 = layer_norm_backward(grad_h1, hat1, inv1, bw[0].astype(F32))
        grad_outputs.append(((grad_x1 + grad_in1) * keep).astype(B16))
        grads = (
            grad_g1,
            grad_query,
            grad_key,
            grad_value,
            grad_out,
            grad_g2,
            grad_cquery,
            grad_ckey,
            grad_cvalue,
            grad_cout,
            grad_g3,
            grad_gate,
            grad_up,
            grad_down,
        )
        part_sum = reduce_grads(grads)
        totals = part_sum if totals is None else tuple((a + b for a, b in zip(totals, part_sum)))
    output = jnp.stack(outputs)[:, None]
    grad_tokens = jnp.stack(grad_outputs)[:, None]
    return (
        output,
        grad_tokens,
        totals[0],
        totals[1],
        totals[2],
        totals[3],
        totals[4],
        totals[5],
        totals[6],
        totals[7],
        totals[8],
        totals[9],
        totals[10],
        totals[11],
        totals[12],
        totals[13],
    )


def solution(mesh):
    return jax.shard_map(
        per_device,
        mesh=mesh,
        in_specs=(
            P(None, "fsdp", "ctx", None),
            P(None, "fsdp", None, None),
            P(None, "fsdp", "ctx", None),
            P(None, "fsdp"),
            P("fsdp"),
            P("fsdp", "tp"),
            P("fsdp", "tp"),
            P("fsdp", "tp"),
            P("tp", "fsdp"),
            P("fsdp"),
            P("fsdp", "tp"),
            P("fsdp", "tp"),
            P("fsdp", "tp"),
            P("tp", "fsdp"),
            P("fsdp"),
            P("fsdp", "tp"),
            P("fsdp", "tp"),
            P("tp", "fsdp"),
        ),
        out_specs=(
            P(None, "fsdp", "ctx", None),
            P(None, "fsdp", "ctx", None),
            P("fsdp"),
            P("fsdp", "tp"),
            P("fsdp", "tp"),
            P("fsdp", "tp"),
            P("tp", "fsdp"),
            P("fsdp"),
            P("fsdp", "tp"),
            P("fsdp", "tp"),
            P("fsdp", "tp"),
            P("tp", "fsdp"),
            P("fsdp"),
            P("fsdp", "tp"),
            P("fsdp", "tp"),
            P("tp", "fsdp"),
        ),
        check_vma=False,
    )
```

profile of v0, /device:TPU:0, one launch (start us, length us, event | category | flops | bytes accessed | tf_op | source)
XLA Modules:
  0.0 3338.7 jit_solution(3638697203139996122)
XLA Ops:
  40.7 21.4 all-gather.25.cloned.1.call-done
  106.7 65.8 %all-gather.27.cloned.1.call-done = bf16[1056,12,64]{2,1,0:T(8,128)(2,1)} async-done(((bf16[264,12,64]{2,1,0:T(8,128)(2,1)}), bf16[1056,12,64]{2,1,0:T(8,128)(2,1)}) %all-gather.27.cloned.1.call-update) | async-done | bytes 1622032 | tf_op jit(solution)/shard_map/all_gather | solution.py:238
  196.0 60.0 %all-gather.21.cloned.1.call-done = bf16[1056,12,64]{2,1,0:T(8,128)(2,1)} async-done(((bf16[264,12,64]{2,1,0:T(8,128)(2,1)}), bf16[1056,12,64]{2,1,0:T(8,128)(2,1)}) %all-gather.21.cloned.1.call-update) | async-done | bytes 1622032 | tf_op jit(solution)/shard_map/all_gather | solution.py:239
  270.4 68.9 %all-gather.47.cloned.1.call-done = bf16[1056,12,64]{2,1,0:T(8,128)(2,1)} async-done(((bf16[264,12,64]{2,1,0:T(8,128)(2,1)}), bf16[1056,12,64]{2,1,0:T(8,128)(2,1)}) %all-gather.47.cloned.1.call-update) | async-done | bytes 1622032 | tf_op jit(solution)/shard_map/all_gather | solution.py:238
  362.2 60.7 %all-gather.45.cloned.1.call-done = bf16[1056,12,64]{2,1,0:T(8,128)(2,1)} async-done(((bf16[264,12,64]{2,1,0:T(8,128)(2,1)}), bf16[1056,12,64]{2,1,0:T(8,128)(2,1)}) %all-gather.45.cloned.1.call-update) | async-done | bytes 1622032 | tf_op jit(solution)/shard_map/all_gather | solution.py:239
  491.2 84.6 %all-reduce.29.cloned.1.call-done = (f32[264,1536]{1,0:T(8,128)}, f32[264,1536]{1,0:T(8,128)}) async-done(((f32[264,1536]{1,0:T(8,128)}, f32[264,1536]{1,0:T(8,128)}), (f32[264,1536]{1,0:T(8,128)}, f32[264,1536]{1,0:T(8,128)})) %all-reduce.29.cloned.1.call-update) | async-done | bytes 3244048 | tf_op jit(solution)/shard_map/psum | solution.py:118
  579.7 21.7 all-gather.33.cloned.1.call-done
  642.2 78.9 %all-reduce.27.cloned.1.call-done = (f32[264,1536]{1,0:T(8,128)}, f32[264,1536]{1,0:T(8,128)}) async-done(((f32[264,1536]{1,0:T(8,128)}, f32[264,1536]{1,0:T(8,128)}), (f32[264,1536]{1,0:T(8,128)}, f32[264,1536]{1,0:T(8,128)})) %all-reduce.27.cloned.1.call-update) | async-done | bytes 3244048 | tf_op jit(solution)/shard_map/psum | solution.py:118
  727.2 59.5 %all-gather.39.cloned.1.call-done = bf16[1536,3072]{1,0:T(8,128)(2,1)} async-done(((bf16[384,3072]{1,0:T(8,128)(2,1)}), bf16[1536,3072]{1,0:T(8,128)(2,1)}) %all-gather.39.cloned.1.call-update) | async-done | bytes 9437200 | tf_op jit(solution)/shard_map/all_gather | solution.py:29
  795.1 57.3 %all-gather.41.cloned.1.call-done = bf16[1536,3072]{1,0:T(8,128)(2,1)} async-done(((bf16[384,3072]{1,0:T(8,128)(2,1)}), bf16[1536,3072]{1,0:T(8,128)(2,1)}) %all-gather.41.cloned.1.call-update) | async-done | bytes 9437200 | tf_op jit(solution)/shard_map/all_gather | solution.py:30
  870.0 48.0 %all-gather.43.cloned.1.call-done = bf16[3072,1536]{1,0:T(8,128)(2,1)} async-done(((bf16[3072,384]{1,0:T(8,128)(2,1)}), bf16[3072,1536]{1,0:T(8,128)(2,1)}) %all-gather.43.cloned.1.call-update) | async-done | bytes 9437200 | tf_op jit(solution)/shard_map/all_gather | solution.py:31
  969.0 88.1 %all-reduce.25.cloned.1.call-done = (f32[264,1536]{1,0:T(8,128)}, f32[264,1536]{1,0:T(8,128)}) async-done(((f32[264,1536]{1,0:T(8,128)}, f32[264,1536]{1,0:T(8,128)}), (f32[264,1536]{1,0:T(8,128)}, f32[264,1536]{1,0:T(8,128)})) %all-reduce.25.cloned.1.call-update) | async-done | bytes 3244048 | tf_op jit(solution)/shard_map/psum | solution.py:122
  1083.0 86.8 %all-reduce.23.cloned.1.call-done = (f32[264,1536]{1,0:T(8,128)}, f32[264,1536]{1,0:T(8,128)}) async-done(((f32[264,1536]{1,0:T(8,128)}, f32[264,1536]{1,0:T(8,128)}), (f32[264,1536]{1,0:T(8,128)}, f32[264,1536]{1,0:T(8,128)})) %all-reduce.23.cloned.1.call-update) | async-done | bytes 3244048 | tf_op jit(solution)/shard_map/psum | solution.py:122
  1523.7 21.3 reduce-scatter.101.cloned.1.call-done
  1547.1 33.1 reduce-scatter.87.cloned.1.call-done
  1582.4 33.3 reduce-scatter.89.cloned.1.call-done
  1617.8 78.5 %reduce-scatter.103.cloned.1.call-done = bf16[384,3072]{1,0:T(8,128)(2,1)} async-done(((bf16[1536,3072]{1,0:T(8,128)(2,1)}), bf16[384,3072]{1,0:T(8,128)(2,1)}) %reduce-scatter.103.cloned.1.call-update) | async-done | bytes 2359312
  1700.5 76.1 %reduce-scatter.105.cloned.1.call-done = bf16[384,3072]{1,0:T(8,128)(2,1)} async-done(((bf16[1536,3072]{1,0:T(8,128)(2,1)}), bf16[384,3072]{1,0:T(8,128)(2,1)}) %reduce-scatter.105.cloned.1.call-update) | async-done | bytes 2359312
  1780.9 31.1 reduce-scatter.67.cloned.1.call-done
  1812.0 35.4 %reduce-scatter.69.cloned.1.call-done = bf16[384,768]{1,0:T(8,128)(2,1)} async-done(((bf16[1536,768]{1,0:T(8,128)(2,1)}), bf16[384,768]{1,0:T(8,128)(2,1)}) %reduce-scatter.69.cloned.1.call-update) | async-done | bytes 589840 | tf_op jit(solution)/shard_map/reduce_scatter | solution.py:74
  1847.4 35.2 %reduce-scatter.63.cloned.1.call-done = bf16[384,768]{1,0:T(8,128)(2,1)} async-done(((bf16[1536,768]{1,0:T(8,128)(2,1)}), bf16[384,768]{1,0:T(8,128)(2,1)}) %reduce-scatter.63.cloned.1.call-update) | async-done | bytes 589840 | tf_op jit(solution)/shard_map/reduce_scatter | solution.py:65
  1882.6 35.2 %reduce-scatter.59.cloned.1.call-done = bf16[384,768]{1,0:T(8,128)(2,1)} async-done(((bf16[1536,768]{1,0:T(8,128)(2,1)}), bf16[384,768]{1,0:T(8,128)(2,1)}) %reduce-scatter.59.cloned.1.call-update) | async-done | bytes 589840 | tf_op jit(solution)/shard_map/reduce_scatter | solution.py:62
  1917.9 36.0 %reduce-scatter.55.cloned.1.call-done = bf16[384,768]{1,0:T(8,128)(2,1)} async-done(((bf16[1536,768]{1,0:T(8,128)(2,1)}), bf16[384,768]{1,0:T(8,128)(2,1)}) %reduce-scatter.55.cloned.1.call-update) | async-done | bytes 589840 | tf_op jit(solution)/shard_map/reduce_scatter | solution.py:59
  1953.8 35.2 %reduce-scatter.65.cloned.1.call-done = bf16[384,768]{1,0:T(8,128)(2,1)} async-done(((bf16[1536,768]{1,0:T(8,128)(2,1)}), bf16[384,768]{1,0:T(8,128)(2,1)}) %reduce-scatter.65.cloned.1.call-update) | async-done | bytes 589840 | tf_op jit(solution)/shard_map/reduce_scatter | solution.py:65
  1989.1 36.0 %reduce-scatter.61.cloned.1.call-done = bf16[384,768]{1,0:T(8,128)(2,1)} async-done(((bf16[1536,768]{1,0:T(8,128)(2,1)}), bf16[384,768]{1,0:T(8,128)(2,1)}) %reduce-scatter.61.cloned.1.call-update) | async-done | bytes 589840 | tf_op jit(solution)/shard_map/reduce_scatter | solution.py:62
  2025.0 36.0 %reduce-scatter.57.cloned.1.call-done = bf16[384,768]{1,0:T(8,128)(2,1)} async-done(((bf16[1536,768]{1,0:T(8,128)(2,1)}), bf16[384,768]{1,0:T(8,128)(2,1)}) %reduce-scatter.57.cloned.1.call-update) | async-done | bytes 589840 | tf_op jit(solution)/shard_map/reduce_scatter | solution.py:59
  2061.0 80.6 %reduce-scatter.71.cloned.1.call-done = bf16[384,3072]{1,0:T(8,128)(2,1)} async-done(((bf16[1536,3072]{1,0:T(8,128)(2,1)}), bf16[384,3072]{1,0:T(8,128)(2,1)}) %reduce-scatter.71.cloned.1.call-update) | async-done | bytes 2359312 | tf_op jit(solution)/shard_map/reduce_scatter | solution.py:89
  2141.5 80.4 %reduce-scatter.75.cloned.1.call-done = bf16[384,3072]{1,0:T(8,128)(2,1)} async-done(((bf16[1536,3072]{1,0:T(8,128)(2,1)}), bf16[384,3072]{1,0:T(8,128)(2,1)}) %reduce-scatter.75.cloned.1.call-update) | async-done | bytes 2359312 | tf_op jit(solution)/shard_map/reduce_scatter | solution.py:92
  2222.0 80.6 %reduce-scatter.73.cloned.1.call-done = bf16[384,3072]{1,0:T(8,128)(2,1)} async-done(((bf16[1536,3072]{1,0:T(8,128)(2,1)}), bf16[384,3072]{1,0:T(8,128)(2,1)}) %reduce-scatter.73.cloned.1.call-update) | async-done | bytes 2359312 | tf_op jit(solution)/shard_map/reduce_scatter | solution.py:89
  2302.5 80.4 %reduce-scatter.77.cloned.1.call-done = bf16[384,3072]{1,0:T(8,128)(2,1)} async-done(((bf16[1536,3072]{1,0:T(8,128)(2,1)}), bf16[384,3072]{1,0:T(8,128)(2,1)}) %reduce-scatter.77.cloned.1.call-update) | async-done | bytes 2359312 | tf_op jit(solution)/shard_map/reduce_scatter | solution.py:92
  2384.8 158.7 %all-reduce.21.cloned.1.call-done = (f32[264,1536]{1,0:T(8,128)}, f32[264,1536]{1,0:T(8,128)}, f32[264,1536]{1,0:T(8,128)}, f32[264,1536]{1,0:T(8,128)}) async-done(((f32[264,1536]{1,0:T(8,128)}, f32[264,1536]{1,0:T(8,128)}, f32[264,1536]{1,0:T(8,128)}, f32[264,1536]{1,0:T(8,128)}), (f32[264,1536]{1,0:T(8,128)}, f32[264,1536]{1,0:T(8,128)}, f32[264,1536]{1,0:T(8,128)}, ...) | async-done | bytes 6488080 | tf_op jit(solution)/shard_map/psum | solution.py:118
  2582.9 724.7 %all-reduce.31.cloned.1.call-done = (bf16[384,768]{1,0:T(8,128)(2,1)}, bf16[384,768]{1,0:T(8,128)(2,1)}, bf16[384,768]{1,0:T(8,128)(2,1)}, bf16[384,768]{1,0:T(8...) async-done(((bf16[384,768]{1,0:T(8,128)(2,1)}, ...) | async-done | bytes 22413328 | tf_op jit(solution)/shard_map/psum | solution.py:101
  (700 shorter events, 790.6 us)
Async XLA Ops:
  92.5 246.9 %all-gather.47.cloned.1.call-start = ((), (), s32[]{:S(2)}) async-start(), calls=%async_computation.40 | async-start | bytes 5406720 | tf_op jit(solution)/shard_map/all_gather | solution.py:238
  95.7 327.3 %all-gather.45.cloned.1.call-start = ((), (), s32[]{:S(2)}) async-start(), calls=%async_computation.39 | async-start | bytes 5406720 | tf_op jit(solution)/shard_map/all_gather | solution.py:239
  100.8 346.2 %all-gather.29.cloned.1.call-start = ((), (), s32[]{:S(2)}) async-start(), calls=%async_computation.31 | async-start | bytes 2949120 | tf_op jit(solution)/shard_map/all_gather | solution.py:22
  101.5 367.0 %all-gather.35.cloned.1.call-start = ((), (), s32[]{:S(2)}) async-start(), calls=%async_computation.34 | async-start | bytes 1474560 | tf_op jit(solution)/shard_map/all_gather | solution.py:25
  102.3 382.7 %all-gather.31.cloned.1.call-start = ((), (), s32[]{:S(2)}) async-start(), calls=%async_computation.32 | async-start | bytes 1474560 | tf_op jit(solution)/shard_map/all_gather | solution.py:26
  102.8 473.0 %all-reduce.29.cloned.1.call-start = ((), (), s32[]{:S(2)}) async-start(), calls=%async_computation.71 | async-start | bytes 6488064 | tf_op jit(solution)/shard_map/psum | solution.py:118
  462.1 259.0 %all-reduce.27.cloned.1.call-start = ((), (), s32[]{:S(2)}) async-start(), calls=%async_computation.70 | async-start | bytes 6488064 | tf_op jit(solution)/shard_map/psum | solution.py:118
  634.2 283.8 %all-gather.43.cloned.1.call-start = ((), (), s32[]{:S(2)}) async-start(), calls=%async_computation.38 | async-start | bytes 11796480 | tf_op jit(solution)/shard_map/all_gather | solution.py:31
  634.8 422.3 %all-reduce.25.cloned.1.call-start = ((), (), s32[]{:S(2)}) async-start(), calls=%async_computation.69 | async-start | bytes 6488064 | tf_op jit(solution)/shard_map/psum | solution.py:122
  1081.7 318.2 %reduce-scatter.81.cloned.1.call-start = ((), (), s32[]{:S(2)}) async-start(), calls=%async_computation.54 | async-start | bytes 2027520 | tf_op jit(solution)/shard_map/convert_element_type | solution.py:356
  1281.6 232.4 %reduce-scatter.95.cloned.1.call-start = ((), (), s32[]{:S(2)}) async-start(), calls=%async_computation.61 | async-start | bytes 1474560
  1289.5 226.4 %reduce-scatter.97.cloned.1.call-start = ((), (), s32[]{:S(2)}) async-start(), calls=%async_computation.62 | async-start | bytes 1474560
  1296.7 221.1 %reduce-scatter.91.cloned.1.call-start = ((), (), s32[]{:S(2)}) async-start(), calls=%async_computation.59 | async-start | bytes 1474560
  1319.1 226.0 %reduce-scatter.101.cloned.1.call-start = ((), (), s32[]{:S(2)}) async-start(), calls=%async_computation.64 | async-start | bytes 2949120
  1328.0 252.2 %reduce-scatter.87.cloned.1.call-start = ((), (), s32[]{:S(2)}) async-start(), calls=%async_computation.57 | async-start | bytes 2949120
  1336.8 278.9 %reduce-scatter.89.cloned.1.call-start = ((), (), s32[]{:S(2)}) async-start(), calls=%async_computation.58 | async-start | bytes 2949120
  1345.6 350.6 %reduce-scatter.103.cloned.1.call-start = ((), (), s32[]{:S(2)}) async-start(), calls=%async_computation.65 | async-start | bytes 11796480
  1367.9 408.8 %reduce-scatter.105.cloned.1.call-start = ((), (), s32[]{:S(2)}) async-start(), calls=%async_computation.66 | async-start | bytes 11796480
  1390.8 421.2 %reduce-scatter.67.cloned.1.call-start = ((), (), s32[]{:S(2)}) async-start(), calls=%async_computation.47 | async-start | bytes 2949120 | tf_op jit(solution)/shard_map/reduce_scatter | solution.py:74
  1395.6 451.8 %reduce-scatter.69.cloned.1.call-start = ((), (), s32[]{:S(2)}) async-start(), calls=%async_computation.48 | async-start | bytes 2949120 | tf_op jit(solution)/shard_map/reduce_scatter | solution.py:74
  1399.8 482.8 %reduce-scatter.63.cloned.1.call-start = ((), (), s32[]{:S(2)}) async-start(), calls=%async_computation.45 | async-start | bytes 2949120 | tf_op jit(solution)/shard_map/reduce_scatter | solution.py:65
  1405.2 512.6 %reduce-scatter.59.cloned.1.call-start = ((), (), s32[]{:S(2)}) async-start(), calls=%async_computation.43 | async-start | bytes 2949120 | tf_op jit(solution)/shard_map/reduce_scatter | solution.py:62
  1430.1 523.7 %reduce-scatter.55.cloned.1.call-start = ((), (), s32[]{:S(2)}) async-start(), calls=%async_computation.41 | async-start | bytes 2949120 | tf_op jit(solution)/shard_map/reduce_scatter | solution.py:59
  1436.9 552.2 %reduce-scatter.65.cloned.1.call-start = ((), (), s32[]{:S(2)}) async-start(), calls=%async_computation.46 | async-start | bytes 2949120 | tf_op jit(solution)/shard_map/reduce_scatter | solution.py:65
  1441.7 583.3 %reduce-scatter.61.cloned.1.call-start = ((), (), s32[]{:S(2)}) async-start(), calls=%async_computation.44 | async-start | bytes 2949120 | tf_op jit(solution)/shard_map/reduce_scatter | solution.py:62
  1446.4 614.5 %reduce-scatter.57.cloned.1.call-start = ((), (), s32[]{:S(2)}) async-start(), calls=%async_computation.42 | async-start | bytes 2949120 | tf_op jit(solution)/shard_map/reduce_scatter | solution.py:59
  1451.5 690.0 %reduce-scatter.71.cloned.1.call-start = ((), (), s32[]{:S(2)}) async-start(), calls=%async_computation.49 | async-start | bytes 11796480 | tf_op jit(solution)/shard_map/reduce_scatter | solution.py:89
  1460.6 761.4 %reduce-scatter.75.cloned.1.call-start = ((), (), s32[]{:S(2)}) async-start(), calls=%async_computation.51 | async-start | bytes 11796480 | tf_op jit(solution)/shard_map/reduce_scatter | solution.py:92
  1469.6 832.9 %reduce-scatter.73.cloned.1.call-start = ((), (), s32[]{:S(2)}) async-start(), calls=%async_computation.50 | async-start | bytes 11796480 | tf_op jit(solution)/shard_map/reduce_scatter | solution.py:89
  1478.9 904.1 %reduce-scatter.77.cloned.1.call-start = ((), (), s32[]{:S(2)}) async-start(), calls=%async_computation.52 | async-start | bytes 11796480 | tf_op jit(solution)/shard_map/reduce_scatter | solution.py:92
  1487.9 1055.7 %all-reduce.21.cloned.1.call-start = ((), (), s32[]{:S(2)}) async-start(), calls=%async_computation.67 | async-start | bytes 12976128 | tf_op jit(solution)/shard_map/psum | solution.py:118
  1513.7 1793.9 %all-reduce.31.cloned.1.call-start = ((), (), s32[]{:S(2)}) async-start(), calls=%async_computation.72 | async-start | bytes 45613056 | tf_op jit(solution)/shard_map/psum | solution.py:101
  (185 other events, 5704.8 us)
Sparse Core Ops, SparseCore 0:
  89.7 82.8 all-gather.26
  174.6 81.3 all-gather.20
  258.0 81.3 all-gather.46
  341.5 81.3 all-gather.44
  487.9 87.9 all-reduce.28
  633.1 87.9 all-reduce.26
  722.5 64.2 all-gather.38
  788.2 64.2 all-gather.40
  853.8 64.0 all-gather.42
  969.1 87.9 all-reduce.24
  1081.8 87.9 all-reduce.22
  1204.8 36.3 reduce-scatter.80
  1249.5 36.5 reduce-scatter.78
  1288.4 35.2 reduce-scatter.82
  1326.0 35.2 reduce-scatter.84
  1476.8 32.8 reduce-scatter.98
  1512.2 32.8 reduce-scatter.100
  1547.4 32.8 reduce-scatter.86
  1582.8 32.8 reduce-scatter.88
  1618.2 77.9 reduce-scatter.102
  1698.7 77.9 reduce-scatter.104
  1779.2 32.8 reduce-scatter.66
  1814.5 32.8 reduce-scatter.68
  1849.8 32.8 reduce-scatter.62
  1921.0 32.8 reduce-scatter.54
  1956.2 32.8 reduce-scatter.64
  2063.6 77.9 reduce-scatter.70
  2144.0 77.9 reduce-scatter.74
  2224.6 77.9 reduce-scatter.72
  2305.0 77.9 reduce-scatter.76
  2386.0 157.5 all-reduce.20
  2550.1 757.4 all-reduce.30
  (15 shorter events, 379.1 us)
where the time goes:
time: 3350 us; the launch traced here: 3340 us
  waiting for transfers between devices  2610 us (78%)
  matrix products  381 us (11%)
  local copies, waits for them, and re-layouts  179 us (5%)
  other arithmetic  105 us (3%)
  blocking collectives  42.5 us (1%)
    psum x1, waiting for transfers between devices, reduce_grads(): lax.psum(shares[1].astype(jnp.bfloat16), 'ctx').astype(jnp.float32)  725 us
    psum x3, waiting for transfers between devices, branch_sum(): return lax.psum(value, 'tp')  322 us
    unnamed x59, waiting for transfers between devices  250 us
    psum x2, waiting for transfers between devices, input_sum(): return lax.psum(value, 'tp')  175 us
    reduce_scatter x2, waiting for transfers between devices, reduce_grads(): lax.psum_scatter(gs[11].astype(jnp.bfloat16), 'fsdp', scatter_dimension=0...  161 us
    reduce_scatter x2, waiting for transfers between devices, reduce_grads(): lax.psum_scatter(gs[12].astype(jnp.bfloat16), 'fsdp', scatter_dimension=0...  161 us
    all_gather x2, waiting for transfers between devices, per_device(): lax.all_gather(keys, 'ctx', axis=0, tiled=True)  135 us
    unnamed x378, local copies, waits for them, and re-layouts  123 us
  transfers between devices with their start and end apart: 47, of which 37 were waited for; matrix products, arithmetic and copies ran while one was open for 15% of the time, Pallas kernels for 0%

commit v1 on v0

v1 whole, which is shorter than its diff:
```python
import functools

import jax
import jax.numpy as jnp
import numpy as np
from jax import lax
from jax.experimental import pallas as pl
from jax.experimental.pallas import tpu as pltpu
from jax.sharding import PartitionSpec as P

HD = 64
ROT = 32
LEN = 1025
F32 = jnp.float32
B16 = jnp.bfloat16
EPS = 1e-05
VMEM_LIMIT = 60 * 1024 * 1024

NN = (((1,), (0,)), ((), ()))
NT = (((1,), (1,)), ((), ()))
TN = (((0,), (0,)), ((), ()))


def dot(a, b, dims=NN):
    return lax.dot_general(a, b, dims, preferred_element_type=F32)


def call(kernel, name, grid, in_specs, out_specs, out_shape, scratch=(), flops=0, bytes_accessed=0, trans=0):
    return pl.pallas_call(
        kernel,
        grid=grid,
        in_specs=in_specs,
        out_specs=out_specs,
        out_shape=out_shape,
        scratch_shapes=list(scratch),
        name=name,
        compiler_params=pltpu.CompilerParams(
            dimension_semantics=("arbitrary",) * len(grid), vmem_limit_bytes=VMEM_LIMIT
        ),
        cost_estimate=pl.CostEstimate(
            flops=int(flops), bytes_accessed=int(bytes_accessed), transcendentals=int(trans)
        ),
    )


def whole(shape):
    zeros = (0,) * len(shape)
    return pl.BlockSpec(shape, lambda *_: zeros)


def shape(dims, kind=B16):
    return jax.ShapeDtypeStruct(dims, kind)


def normalized(v):
    cent = v - jnp.mean(v, -1, keepdims=True)
    inv = lax.rsqrt(jnp.mean(cent * cent, -1, keepdims=True) + EPS)
    return cent * inv, inv


def norm_back(dn, hat, inv, gain):
    dxh = dn * gain
    grad = inv * (
        dxh - jnp.mean(dxh, -1, keepdims=True) - hat * jnp.mean(dxh * hat, -1, keepdims=True)
    )
    return grad, jnp.sum(dn * hat, 0, keepdims=True)


def turned(v, cos, lo, hi):
    wide = v.shape[-1]
    half = ROT // 2
    return v * cos + pltpu.roll(v, wide - half, 1) * lo + pltpu.roll(v, half, 1) * hi


def qkv_kernel(tiles, x_ref, g_ref, w_ref, cos_ref, lo_ref, hi_ref, h_out, q_out, kv_out, h_s):
    j = pl.program_id(0)

    @pl.when(j == 0)
    def _():
        hat, _ = normalized(x_ref[...].astype(F32))
        h = (hat * g_ref[...]).astype(B16)
        h_s[...] = h
        h_out[...] = h

    acc = dot(h_s[...], w_ref[...])

    @pl.when(j < tiles)
    def _():
        q_out[...] = turned(acc, cos_ref[...], lo_ref[...], hi_ref[...]).astype(B16)

    @pl.when(jnp.logical_and(j >= tiles, j < 2 * tiles))
    def _():
        kv_out[...] = turned(acc, cos_ref[...], lo_ref[...], hi_ref[...]).astype(B16)

    @pl.when(j >= 2 * tiles)
    def _():
        kv_out[...] = acc.astype(B16)


def qkv_proj(x, gain, w, tables):
    rows, d = x.shape
    inner = w.shape[1] // 3
    bc = 384
    tiles = inner // bc
    return call(
        functools.partial(qkv_kernel, tiles),
        "qkv_proj",
        (3 * tiles,),
        [
            whole((rows, d)),
            whole((1, d)),
            pl.BlockSpec((d, bc), lambda j: (0, j)),
            whole((rows, bc)),
            whole((rows, bc)),
            whole((rows, bc)),
        ],
        [
            whole((rows, d)),
            pl.BlockSpec((rows, bc), lambda j: (0, jnp.minimum(j, tiles - 1))),
            pl.BlockSpec((rows, bc), lambda j: (0, jnp.maximum(j - tiles, 0))),
        ],
        [shape((rows, d)), shape((rows, inner)), shape((rows, 2 * inner))],
        [pltpu.VMEM((rows, d), B16)],
        2 * rows * d * 3 * inner,
        2 * (2 * rows * d + d * 3 * inner + rows * 3 * inner),
    )(x, gain, w, *tables)


def attn_kernel(n, q_ref, k_ref, v_ref, bias_ref, w_ref, att_out, lse_out, part_out, acc):
    j = pl.program_id(0)
    bias = bias_ref[...]
    outs = []
    lses = []
    for a in range(2):
        lanes = slice(a * HD, (a + 1) * HD)
        qh = q_ref[:, lanes] * jnp.asarray(HD**-0.5, B16)
        s = dot(qh, k_ref[:, lanes], NT) + bias
        top = jnp.max(s, -1, keepdims=True)
        e = jnp.exp(s - top)
        total = jnp.sum(e, -1, keepdims=True)
        outs.append(dot(e.astype(B16), v_ref[:, lanes]) / total)
        lses.append(jnp.broadcast_to(top + jnp.log(total), (s.shape[0], HD)))
    att = jnp.concatenate(outs, 1).astype(B16)
    att_out[...] = att
    lse_out[0] = jnp.concatenate(lses, 1)
    term = dot(att, w_ref[...], NT)

    @pl.when(j == 0)
    def _():
        acc[...] = term

    @pl.when(j > 0)
    def _():
        acc[...] += term

    @pl.when(j == n - 1)
    def _():
        part_out[...] = acc[...].astype(B16)


def attention(q, kv, bias, wo_t):
    rows, inner = q.shape
    keys = kv.shape[0]
    d = wo_t.shape[0]
    n = inner // 128
    return call(
        functools.partial(attn_kernel, n),
        "attention",
        (n,),
        [
            pl.BlockSpec((rows, 128), lambda j: (0, j)),
            pl.BlockSpec((keys, 128), lambda j: (0, j)),
            pl.BlockSpec((keys, 128), lambda j: (0, n + j)),
            whole((1, keys)),
            pl.BlockSpec((d, 128), lambda j: (0, j)),
        ],
        [
            pl.BlockSpec((rows, 128), lambda j: (0, j)),
            pl.BlockSpec((1, rows, 128), lambda j: (j, 0, 0)),
            whole((rows, d)),
        ],
        [shape((rows, inner)), shape((n, rows, 128), F32), shape((rows, d))],
        [pltpu.VMEM((rows, d), F32)],
        4 * rows * keys * inner * 4 + 2 * rows * d * inner,
        2 * (2 * rows * inner + 2 * keys * inner + d * inner + rows * d),
        rows * keys * inner // HD,
    )(q, kv, kv, bias, wo_t)


def cross_kernel(
    n, x_ref, a_ref, b_ref, g_ref, wq_ref, ck_ref, cv_ref, wo_ref,
    x1_out, h_out, cq_out, catt_out, part_out, h_s, acc,
):
    j = pl.program_id(0)

    @pl.when(j == 0)
    def _():
        x1 = x_ref[...].astype(F32) + (a_ref[...].astype(F32) + b_ref[...].astype(F32))
        x1_out[...] = x1
        hat, _ = normalized(x1)
        h = (hat * g_ref[...]).astype(B16)
        h_s[...] = h
        h_out[...] = h

    cq = dot(h_s[...], wq_ref[...]).astype(B16)
    cq_out[...] = cq
    outs = []
    for a in range(cq.shape[1] // HD):
        lanes = slice(a * HD, (a + 1) * HD)
        s = dot(cq[:, lanes] * jnp.asarray(HD**-0.5, B16), ck_ref[:, lanes], NT)
        e = jnp.exp(s - jnp.max(s, -1, keepdims=True))
        total = jnp.sum(e, -1, keepdims=True)
        outs.append(dot(e.astype(B16), cv_ref[:, lanes]) / total)
    catt = jnp.concatenate(outs, 1).astype(B16)
    catt_out[...] = catt
    term = dot(catt, wo_ref[...], NT)

    @pl.when(j == 0)
    def _():
        acc[...] = term

    @pl.when(j > 0)
    def _():
        acc[...] += term

    @pl.when(j == n - 1)
    def _():
        part_out[...] = acc[...].astype(B16)


def cross(x, pa, pb, gain, wcq, ckv, wco_t):
    rows, d = x.shape
    inner = wcq.shape[1]
    cond = ckv.shape[0]
    bc = 256
    n = inner // bc
    col = pl.BlockSpec((rows, bc), lambda j: (0, j))
    return call(
        functools.partial(cross_kernel, n),
        "cross",
        (n,),
        [
            whole((rows, d)),
            whole((rows, d)),
            whole((rows, d)),
            whole((1, d)),
            pl.BlockSpec((d, bc), lambda j: (0, j)),
            pl.BlockSpec((cond, bc), lambda j: (0, j)),
            pl.BlockSpec((cond, bc), lambda j: (0, n + j)),
            pl.BlockSpec((d, bc), lambda j: (0, j)),
        ],
        [whole((rows, d)), whole((rows, d)), col, col, whole((rows, d))],
        [
            shape((rows, d), F32),
            shape((rows, d)),
            shape((rows, inner)),
            shape((rows, inner)),
            shape((rows, d)),
        ],
        [pltpu.VMEM((rows, d), B16), pltpu.VMEM((rows, d), F32)],
        4 * rows * d * inner + 4 * rows * cond * inner * 2,
        2 * (7 * rows * d + 2 * d * inner),
        rows * cond * inner // HD,
    )(x, pa, pb, gain, wcq, ckv, ckv, wco_t)


def mlp_kernel(
    n, micro, *refs
):
    (x1_refs, a_refs, b_refs) = (refs[:micro], refs[micro : 2 * micro], refs[2 * micro : 3 * micro])
    (g_ref, gy_ref, wg_ref, wu_ref, wd_ref, x2_out, h_out, hid_out, dg_out, du_out, y_out, dh_out,
     h_s, y_s, dh_s) = refs[3 * micro :]
    j = pl.program_id(0)
    rows = x1_refs[0].shape[0]

    @pl.when(j == 0)
    def _():
        for m in range(micro):
            part = pl.ds(m * rows, rows)
            x2 = x1_refs[m][...] + (a_refs[m][...].astype(F32) + b_refs[m][...].astype(F32))
            x2_out[part, :] = x2
            hat, _ = normalized(x2)
            h = (hat * g_ref[...]).astype(B16)
            h_s[part, :] = h
            h_out[part, :] = h

    h = h_s[...]
    gate = dot(h, wg_ref[...])
    up = dot(h, wu_ref[...])
    dhid = dot(gy_ref[...], wd_ref[...])
    sig = jax.nn.sigmoid(gate)
    act = gate * sig
    hid = (act * up).astype(B16)
    dg = (dhid * up * sig * (1.0 + gate * (1.0 - sig))).astype(B16)
    du = (dhid * act).astype(B16)
    hid_out[...] = hid
    dg_out[...] = dg
    du_out[...] = du
    y = dot(hid, wd_ref[...], NT)
    dh = dot(dg, wg_ref[...], NT) + dot(du, wu_ref[...], NT)

    @pl.when(j == 0)
    def _():
        y_s[...] = y
        dh_s[...] = dh

    @pl.when(j > 0)
    def _():
        y_s[...] += y
        dh_s[...] += dh

    @pl.when(j == n - 1)
    def _():
        y_out[...] = y_s[...].astype(B16)
        dh_out[...] = dh_s[...].astype(B16)


def mlp(x1s, pas, pbs, gain, gyb, wg, wu, wd_t):
    micro = len(x1s)
    rows, d = x1s[0].shape
    total = micro * rows
    hidden = wg.shape[1]
    bc = 256
    n = hidden // bc
    once = lambda s: pl.BlockSpec(s, lambda j: (0, 0), pipeline_mode=pl.Buffered(1))
    wcol = pl.BlockSpec((d, bc), lambda j: (0, j))
    ocol = pl.BlockSpec((total, bc), lambda j: (0, j))
    return call(
        functools.partial(mlp_kernel, n, micro),
        "mlp",
        (n,),
        [once((rows, d))] * (3 * micro)
        + [whole((1, d)), once((total, d)), wcol, wcol, wcol],
        [once((total, d)), once((total, d)), ocol, ocol, ocol, once((total, d)), once((total, d))],
        [
            shape((total, d), F32),
            shape((total, d)),
            shape((total, hidden)),
            shape((total, hidden)),
            shape((total, hidden)),
            shape((total, d)),
            shape((total, d)),
        ],
        [pltpu.VMEM((total, d), B16), pltpu.VMEM((total, d), F32), pltpu.VMEM((total, d), F32)],
        12 * total * d * hidden,
        2 * (3 * d * hidden + 3 * total * hidden + 10 * total * d),
        total * hidden,
    )(*x1s, *pas, *pbs, gain, gyb, wg, wu, wd_t)


def cross_back_kernel(
    n, x2_ref, gy_ref, a_ref, b_ref, g_ref, cq_ref, ck_ref, cv_ref, wo_ref, wq_ref,
    g2x_out, gc_out, gg_out, dcq_out, dck_out, dcv_out, part_out, gc_s, acc,
):
    j = pl.program_id(0)

    @pl.when(j == 0)
    def _():
        hat, inv = normalized(x2_ref[...])
        dn = a_ref[...].astype(F32) + b_ref[...].astype(F32)
        grad, gg = norm_back(dn, hat, inv, g_ref[...])
        gg_out[...] = gg
        g2x = gy_ref[...].astype(F32) + grad
        g2x_out[...] = g2x
        gc = g2x.astype(B16)
        gc_s[...] = gc
        gc_out[...] = gc

    dca = dot(gc_s[...], wo_ref[...]).astype(B16)
    dqs = []
    dks = []
    dvs = []
    for a in range(dca.shape[1] // HD):
        lanes = slice(a * HD, (a + 1) * HD)
        cqh = cq_ref[:, lanes] * jnp.asarray(HD**-0.5, B16)
        ckh = ck_ref[:, lanes]
        s = dot(cqh, ckh, NT)
        e = jnp.exp(s - jnp.max(s, -1, keepdims=True))
        p = e / jnp.sum(e, -1, keepdims=True)
        dp = dot(dca[:, lanes], cv_ref[:, lanes], NT)
        ds = (p * (dp - jnp.sum(p * dp, -1, keepdims=True))).astype(B16)
        dqs.append(dot(ds, ckh) * HD**-0.5)
        dks.append(dot(ds, cqh, TN))
        dvs.append(dot(p.astype(B16), dca[:, lanes], TN))
    dcq = jnp.concatenate(dqs, 1).astype(B16)
    dcq_out[...] = dcq
    dck_out[...] = jnp.concatenate(dks, 1).astype(B16)
    dcv_out[...] = jnp.concatenate(dvs, 1).astype(B16)
    term = dot(dcq, wq_ref[...], NT)

    @pl.when(j == 0)
    def _():
        acc[...] = term

    @pl.when(j > 0)
    def _():
        acc[...] += term

    @pl.when(j == n - 1)
    def _():
        part_out[...] = acc[...].astype(B16)


def cross_back(m, x2, gyb, pa, pb, gain, cq, ckv, wco_t, wcq):
    rows, inner = cq.shape
    d = x2.shape[1]
    cond = ckv.shape[0]
    bc = 256
    n = inner // bc
    row = pl.BlockSpec((rows, d), lambda j: (m, 0))
    col = pl.BlockSpec((rows, bc), lambda j: (0, j))
    ccol = pl.BlockSpec((cond, bc), lambda j: (0, j))
    wcol = pl.BlockSpec((d, bc), lambda j: (0, j))
    return call(
        functools.partial(cross_back_kernel, n),
        "cross_back",
        (n,),
        [
            row,
            row,
            whole((rows, d)),
            whole((rows, d)),
            whole((1, d)),
            col,
            ccol,
            pl.BlockSpec((cond, bc), lambda j: (0, n + j)),
            wcol,
            wcol,
        ],
        [whole((rows, d)), whole((rows, d)), whole((1, d)), col, ccol, ccol, whole((rows, d))],
        [
            shape((rows, d), F32),
            shape((rows, d)),
            shape((1, d), F32),
            shape((rows, inner)),
            shape((cond, inner)),
            shape((cond, inner)),
            shape((rows, d)),
        ],
        [pltpu.VMEM((rows, d), B16), pltpu.VMEM((rows, d), F32)],
        4 * rows * d * inner + 10 * rows * cond * inner * 2,
        2 * (10 * rows * d + 2 * d * inner),
        rows * cond * inner // HD,
    )(x2, gyb, pa, pb, gain, cq, ckv, ckv, wco_t, wcq)


def attn_back_kernel(
    x1_ref, g2x_ref, a_ref, b_ref, g_ref, wo_ref, q_ref, k_ref, v_ref, lse_ref, bias_ref,
    cos_ref, lo_ref, hi_ref,
    g1x_out, ga_out, gg_out, dq_out, dk_out, dv_out, ga_s,
):
    j = pl.program_id(0)

    @pl.when(j == 0)
    def _():
        hat, inv = normalized(x1_ref[...])
        dn = a_ref[...].astype(F32) + b_ref[...].astype(F32)
        grad, gg = norm_back(dn, hat, inv, g_ref[...])
        gg_out[...] = gg
        g1x = g2x_ref[...] + grad
        g1x_out[...] = g1x
        ga = g1x.astype(B16)
        ga_s[...] = ga
        ga_out[...] = ga

    datt = dot(ga_s[...], wo_ref[...]).astype(B16)
    bias = bias_ref[...]
    dqs = []
    dks = []
    dvs = []
    for a in range(2):
        lanes = slice(a * HD, (a + 1) * HD)
        qh = q_ref[:, lanes] * jnp.asarray(HD**-0.5, B16)
        kh = k_ref[:, lanes]
        s = dot(qh, kh, NT) + bias
        p = jnp.exp(s - lse_ref[0, :, a * HD : a * HD + 1])
        dp = dot(datt[:, lanes], v_ref[:, lanes], NT)
        ds = (p * (dp - jnp.sum(p * dp, -1, keepdims=True))).astype(B16)
        dqs.append(dot(ds, kh) * HD**-0.5)
        dks.append(dot(ds, qh, TN))
        dvs.append(dot(p.astype(B16), datt[:, lanes], TN))
    dq = jnp.concatenate(dqs, 1)
    dq_out[...] = turned(dq, cos_ref[...], -lo_ref[...], -hi_ref[...]).astype(B16)
    dk_out[...] = jnp.concatenate(dks, 1).astype(B16)
    dv_out[...] = jnp.concatenate(dvs, 1).astype(B16)


def attention_back(x1, g2x, pa, pb, gain, wo_t, q, kv, lse, bias, tables):
    rows, inner = q.shape
    d = x1.shape[1]
    keys = kv.shape[0]
    n = inner // 128
    col = pl.BlockSpec((rows, 128), lambda j: (0, j))
    kcol = pl.BlockSpec((keys, 128), lambda j: (0, j))
    return call(
        attn_back_kernel,
        "attention_back",
        (n,),
        [
            whole((rows, d)),
            whole((rows, d)),
            whole((rows, d)),
            whole((rows, d)),
            whole((1, d)),
            pl.BlockSpec((d, 128), lambda j: (0, j)),
            col,
            kcol,
            pl.BlockSpec((keys, 128), lambda j: (0, n + j)),
            pl.BlockSpec((1, rows, 128), lambda j: (j, 0, 0)),
            whole((1, keys)),
            pl.BlockSpec((rows, 128), lambda j: (0, 0)),
            pl.BlockSpec((rows, 128), lambda j: (0, 0)),
            pl.BlockSpec((rows, 128), lambda j: (0, 0)),
        ],
        [whole((rows, d)), whole((rows, d)), whole((1, d)), col, kcol, kcol],
        [
            shape((rows, d), F32),
            shape((rows, d)),
            shape((1, d), F32),
            shape((rows, inner)),
            shape((keys, inner)),
            shape((keys, inner)),
        ],
        [pltpu.VMEM((rows, d), B16)],
        10 * rows * keys * inner * 4 + 2 * rows * d * inner,
        2 * (8 * rows * d + 4 * keys * inner + d * inner),
        rows * keys * inner // HD,
    )(x1, g2x, pa, pb, gain, wo_t, q, kv, kv, lse, bias, *tables)


def qkv_back_kernel(n, tiles, dq_ref, dk_ref, dv_ref, w_ref, cos_ref, lo_ref, hi_ref, all_out, part_out, t_s, acc):
    j = pl.program_id(0)

    @pl.when(j < tiles)
    def _():
        t_s[...] = dq_ref[...]

    @pl.when(jnp.logical_and(j >= tiles, j < 2 * tiles))
    def _():
        t_s[...] = turned(
            dk_ref[...].astype(F32), cos_ref[...], -lo_ref[...], -hi_ref[...]
        ).astype(B16)

    @pl.when(j >= 2 * tiles)
    def _():
        t_s[...] = dv_ref[...]

    all_out[...] = t_s[...]
    term = dot(t_s[...], w_ref[...], NT)

    @pl.when(j == 0)
    def _():
        acc[...] = term

    @pl.when(j > 0)
    def _():
        acc[...] += term

    @pl.when(j == n - 1)
    def _():
        part_out[...] = acc[...].astype(B16)


def qkv_back(dq, dk, dv, w, tables):
    rows, inner = dq.shape
    d = w.shape[0]
    bc = 384
    tiles = inner // bc
    n = 3 * tiles
    last = tiles - 1
    return call(
        functools.partial(qkv_back_kernel, n, tiles),
        "qkv_back",
        (n,),
        [
            pl.BlockSpec((rows, bc), lambda j: (0, jnp.minimum(j, last))),
            pl.BlockSpec((rows, bc), lambda j: (0, jnp.clip(j - tiles, 0, last))),
            pl.BlockSpec((rows, bc), lambda j: (0, jnp.clip(j - 2 * tiles, 0, last))),
            pl.BlockSpec((d, bc), lambda j: (0, j)),
            whole((rows, bc)),
            whole((rows, bc)),
            whole((rows, bc)),
        ],
        [pl.BlockSpec((rows, bc), lambda j: (0, j)), whole((rows, d))],
        [shape((rows, 3 * inner)), shape((rows, d))],
        [pltpu.VMEM((rows, bc), B16), pltpu.VMEM((rows, d), F32)],
        2 * rows * d * 3 * inner,
        2 * (6 * rows * inner + d * 3 * inner + rows * d),
    )(dq, dk, dv, w, *tables)


def input_back_kernel(x_ref, g1x_ref, a_ref, b_ref, g_ref, keep_ref, gx_out, gg_out):
    hat, inv = normalized(x_ref[...].astype(F32))
    dn = a_ref[...].astype(F32) + b_ref[...].astype(F32)
    grad, gg = norm_back(dn, hat, inv, g_ref[...])
    gg_out[...] = gg
    gx_out[...] = ((g1x_ref[...] + grad) * keep_ref[...]).astype(B16)


def input_back(x, g1x, pa, pb, gain, keep):
    rows, d = x.shape
    return call(
        input_back_kernel,
        "input_back",
        (1,),
        [whole((rows, d))] * 4 + [whole((1, d)), whole((rows, 1))],
        [whole((rows, d)), whole((1, d))],
        [shape((rows, d)), shape((1, d), F32)],
        (),
        0,
        14 * rows * d,
    )(x, g1x, pa, pb, gain, keep)


def wgrad_kernel(k, order_ref, *refs):
    out = refs[-1]
    total = dot(refs[0][...], refs[k][...], TN)
    for i in range(1, k):
        total += dot(refs[i][...], refs[k + i][...], TN)
    out[...] = total.astype(B16)


def weight_grad(lefts, rights, order, rb, bc=768):
    k = len(lefts)
    rows, d = lefts[0].shape
    cols = rights[0].shape[1]
    bc = min(bc, cols)
    return pl.pallas_call(
        functools.partial(wgrad_kernel, k),
        grid_spec=pltpu.PrefetchScalarGridSpec(
            num_scalar_prefetch=1,
            grid=(cols // bc, d // rb),
            in_specs=[pl.BlockSpec((rows, rb), lambda j, o, t: (0, t[o]))] * k
            + [pl.BlockSpec((rows, bc), lambda j, o, t: (0, j))] * k,
            out_specs=pl.BlockSpec((rb, bc), lambda j, o, t: (o, j)),
        ),
        out_shape=shape((d, cols)),
        name="weight_grad",
        compiler_params=pltpu.CompilerParams(
            dimension_semantics=("arbitrary", "arbitrary"), vmem_limit_bytes=VMEM_LIMIT
        ),
        cost_estimate=pl.CostEstimate(
            flops=2 * k * rows * d * cols,
            bytes_accessed=2 * (k * rows * (d * (cols // bc) + cols) + d * cols),
            transcendentals=0,
        ),
    )(order, *lefts, *rights)


def swap(v, axis, bit):
    n = lax.axis_size(axis)
    return lax.ppermute(v, axis, [(i, i ^ bit) for i in range(n)])


def scatter_sum(v, n):
    bit = 1
    while bit < n:
        half = v.shape[0] // 2
        v = v[:half] + swap(v[half:], "fsdp", bit)
        bit *= 2
    return v


def xor_order(n):
    order = [0]
    bit = n // 2
    while bit:
        order = order + [o ^ bit for o in order]
        bit //= 2
    return order


def line_sum(v):
    z = lax.axis_index("ctx")
    left = z == 1
    half = v.shape[0] // 2
    v = v + lax.ppermute(v, "ctx", [(0, 1), (3, 2)])
    top, low = v[:half], v[half:]
    got = lax.ppermute(jnp.where(left, low, top), "ctx", [(1, 2), (2, 1)])
    mine = jnp.where(left, top, low) + got
    other = lax.ppermute(mine, "ctx", [(1, 2), (2, 1)])
    full = jnp.concatenate([jnp.where(left, mine, other), jnp.where(left, other, mine)], 0)
    out = lax.ppermute(full, "ctx", [(1, 0), (2, 3)])
    return jnp.where((z == 1) | (z == 2), full, out)


def per_device(
    tokens, conditioning, cotangent, live,
    gain_attn, w_query, w_key, w_value, w_out,
    gain_cross, w_cquery, w_ckey, w_cvalue, w_cout,
    gain_mlp, w_gate, w_up, w_down,
):
    micro = tokens.shape[0]
    blk = tokens.shape[2]
    d = tokens.shape[3]
    rows = -(-blk // 16) * 16
    inner = w_query.shape[1]
    cond_rows = conditioning.shape[2]
    nf = lax.axis_size("fsdp")
    me = lax.axis_index("fsdp")
    ctx_count = lax.axis_size("ctx")
    here = lax.axis_index("ctx")
    base = LEN // ctx_count
    extra = LEN % ctx_count
    first = here * base + jnp.minimum(here, extra)
    own = base + (here < extra).astype(jnp.int32)
    idx = jnp.arange(rows, dtype=jnp.int32)
    row_ok = idx < own
    position = (first + idx).astype(F32)
    slots = np.arange(rows * ctx_count)
    ok = slots % rows < base + (slots // rows < extra)
    bias = jnp.asarray(np.where(ok, 0.0, -1e30).astype(np.float32))[None, :]
    half = ROT // 2
    lane = np.arange(384) % HD
    freq = 10000.0 ** (-np.arange(half, dtype=np.float64) * 2.0 / ROT)
    per_lane = jnp.asarray(np.where(lane < ROT, freq[lane % half], 0.0).astype(np.float32))
    angle = position[:, None] * per_lane[None, :]
    sine = jnp.sin(angle)
    tables = (
        jnp.cos(angle),
        jnp.where(jnp.asarray(lane < half)[None, :], -sine, 0.0),
        jnp.where(jnp.asarray((lane >= half) & (lane < ROT))[None, :], sine, 0.0),
    )

    def gather(w):
        return lax.all_gather(w, "fsdp", axis=0, tiled=True)

    w_qkv = gather(jnp.concatenate([w_query, w_key, w_value], 1))
    gains = gather(jnp.stack([gain_attn, gain_cross, gain_mlp], 1)).astype(F32).T
    wo_t, wcq, wco_t = jnp.split(
        gather(jnp.concatenate([w_out.T, w_cquery, w_cout.T], 1)), 3, axis=1
    )
    w_ckv = gather(jnp.concatenate([w_ckey, w_cvalue], 1))
    wg = gather(w_gate)
    wu = gather(w_up)
    wd_t = gather(w_down.T)
    g1, g2, g3 = gains[0:1], gains[1:2], gains[2:3]

    pad = ((0, 0), (0, rows - blk), (0, 0))
    x_all = jnp.pad(tokens[:, 0], pad)
    xs = [x_all[m] for m in range(micro)]
    keeps = [(row_ok & (live[m, 0] > 0)).astype(F32)[:, None] for m in range(micro)]
    gyb = (
        jnp.pad(cotangent[:, 0], pad).astype(F32) * jnp.stack(keeps)
    ).astype(B16).reshape(micro * rows, d)
    conds = [conditioning[m, 0] for m in range(micro)]

    def tp(v):
        return swap(v, "tp", 1)

    h1s, qs, kvs = [], [], []
    for m in range(micro):
        h1, q, kv = qkv_proj(xs[m], g1, w_qkv, tables)
        h1s.append(h1)
        qs.append(q)
        kvs.append(lax.all_gather(kv, "ctx", axis=0, tiled=True))
    ckvs = [jnp.dot(conds[m], w_ckv, preferred_element_type=F32).astype(B16) for m in range(micro)]
    atts, lses, x1s, h2s, cqs, catts, pas, pbs = [], [], [], [], [], [], [], []
    for m in range(micro):
        att, lse, part = attention(qs[m], kvs[m], bias, wo_t)
        x1, h2, cq, catt, part2 = cross(xs[m], part, tp(part), g2, wcq, ckvs[m], wco_t)
        atts.append(att)
        lses.append(lse)
        x1s.append(x1)
        h2s.append(h2)
        cqs.append(cq)
        catts.append(catt)
        pas.append(part2)
        pbs.append(tp(part2))
    x2, h3, hid, dg, du, y_part, dh_part = mlp(x1s, pas, pbs, g3, gyb, wg, wu, wd_t)
    y_other = tp(y_part)
    result = x2 + (y_part.astype(F32) + y_other.astype(F32))
    output = (result.reshape(micro, rows, d) * jnp.stack(keeps)).astype(B16)[:, None, :blk]

    if (d // nf) % 128 == 0:
        order = (me ^ jnp.asarray(xor_order(nf), jnp.int32)).astype(jnp.int32)
        rb = d // nf
        arranged = lambda h: h
    else:
        rb = 384
        order = jnp.arange(d // rb, dtype=jnp.int32)
        piece = d // nf

        def arranged(h):
            return jnp.concatenate(
                [
                    lax.dynamic_slice_in_dim(h, (me ^ o) * piece, piece, 1)
                    for o in xor_order(nf)
                ],
                1,
            )

    def reduced(lefts, rights):
        g = weight_grad([arranged(h) for h in lefts], rights, order, rb)
        return line_sum(scatter_sum(g, nf)).astype(F32)

    grad_down = reduced([gyb], [hid]).T
    grad_gate = reduced([h3], [dg])
    grad_up = reduced([h3], [du])

    gcs, gg3s, dcqs, dckvs, gas, gg2s, gg1s, dqkvs, gxs = [], [], [], [], [], [], [], [], []
    for m in range(micro):
        dha = dh_part[m * rows : (m + 1) * rows]
        g2x, gc, gg3, dcq, dck, dcv, part3 = cross_back(
            m, x2, gyb, dha, tp(dha), g3, cqs[m], ckvs[m], wco_t, wcq
        )
        g1x, ga, gg2, dq, dk, dv = attention_back(
            x1s[m], g2x, part3, tp(part3), g2, wo_t, qs[m], kvs[m], lses[m], bias, tables
        )
        dkv = lax.psum_scatter(
            jnp.concatenate([dk, dv], 1), "ctx", scatter_dimension=0, tiled=True
        )
        dqkv, part4 = qkv_back(dq, dkv[:, :inner], dkv[:, inner:], w_qkv, tables)
        gx, gg1 = input_back(xs[m], g1x, part4, tp(part4), g1, keeps[m])
        gcs.append(gc)
        gg3s.append(gg3)
        dcqs.append(dcq)
        dckvs.append(jnp.concatenate([dck, dcv], 1))
        gas.append(ga)
        gg2s.append(gg2)
        dqkvs.append(dqkv)
        gg1s.append(gg1)
        gxs.append(gx)
    grad_tokens = jnp.stack(gxs)[:, None, :blk]

    grad_cout = reduced(gcs, catts).T
    grad_cquery = reduced(h2s, dcqs)
    cond_cat = jnp.concatenate(conds, 0)
    cpiece = cond_cat.shape[1] // nf
    cond_cat = jnp.concatenate(
        [lax.dynamic_slice_in_dim(cond_cat, (me ^ o) * cpiece, cpiece, 1) for o in xor_order(nf)], 1
    )
    grad_ckv = jnp.einsum(
        "rc,rk->ck", cond_cat, jnp.concatenate(dckvs, 0), preferred_element_type=F32
    ).astype(B16)
    grad_ckv = line_sum(scatter_sum(grad_ckv, nf)).astype(F32)
    grad_out = reduced(gas, atts).T
    grad_qkv = reduced(h1s, dqkvs)
    gg = jnp.concatenate([sum(gg1s), sum(gg2s), sum(gg3s)], 0)
    gg = lax.psum(gg, ("fsdp", "ctx"))
    gg = lax.dynamic_slice_in_dim(gg, me * (d // nf), d // nf, 1)
    return (
        output,
        grad_tokens,
        gg[0],
        grad_qkv[:, :inner],
        grad_qkv[:, inner : 2 * inner],
        grad_qkv[:, 2 * inner :],
        grad_out,
        gg[1],
        grad_cquery,
        grad_ckv[:, :inner],
        grad_ckv[:, inner:],
        grad_cout,
        gg[2],
        grad_gate,
        grad_up,
        grad_down,
    )


def solution(mesh):
    acts = P(None, "fsdp", "ctx", None)
    rows = P("fsdp", "tp")
    cols = P("tp", "fsdp")
    vec = P("fsdp")
    weights = (vec, rows, rows, rows, cols, vec, rows, rows, rows, cols, vec, rows, rows, cols)
    return jax.shard_map(
        per_device,
        mesh=mesh,
        in_specs=(acts, P(None, "fsdp", None, None), acts, P(None, "fsdp")) + weights,
        out_specs=(acts, acts) + weights,
        check_vma=False,
    )
```

time: 3350 us -> 1560 us (0.47)
  waiting for transfers between devices: 2610 us -> 816 us
  matrix products: 381 us -> 5.96 us
  Pallas kernels: 0 us -> 331 us
  local copies, waits for them, and re-layouts: 179 us -> 75.1 us
  starting transfers between devices: 4.05 us -> 107 us
  blocking collectives: 42.5 us -> 104 us
    psum x6 -> x0, waiting for transfers between devices: 1220 us -> none  [the longest x1 725 us: reduce_grads(): lax.psum(shares[1].astype(jnp.bfloat16), 'ctx').astype(jnp.float32)]
    reduce_scatter x12 -> x2, waiting for transfers between devices: 602 us -> 0.01 us  [per_device(): lax.psum_scatter(jnp.concatenate([dk, dv], 1), 'ctx', scatter_dimension=0...]
    ppermute x0 -> x59, waiting for transfers between devices: none -> 468 us  [the longest x8 197 us: line_sum(): out = lax.ppermute(full, 'ctx', [(1, 0), (2, 3)])]
    dot_general x84 -> x3, matrix products: 377 us -> 5.96 us  [the longest x2 4.35 us: per_device(): jnp.dot(conds[m], w_ckv, preferred_element_type=F32).astype(B16)]
    pallas_call x0 -> x22, Pallas kernels: none -> 331 us  [the longest x7 91.8 us: weight_grad(): pl.pallas_call(functools.partial(wgrad_kernel, k), grid_spec=pltpu.Prefet...]
    unnamed x59 -> x10, waiting for transfers between devices: 250 us -> 1.52 us
    all_gather x15 -> x8, waiting for transfers between devices: 535 us -> 347 us  [the longest x6 234 us: gather(): return lax.all_gather(w, 'fsdp', axis=0, tiled=True)]
    ppermute x0 -> x59, starting transfers between devices: none -> 107 us  [the longest x8 60.4 us: line_sum(): v = v + lax.ppermute(v, 'ctx', [(0, 1), (3, 2)])]
  transfers between devices with their start and end apart: 47 -> 69, of which waited for: 37 -> 28; matrix products, arithmetic and copies ran while one was open for 15% -> 10% of each run, Pallas kernels for 0% -> 15%
where the time goes in v1:
time: 1560 us; the launch traced here: 1550 us
  waiting for transfers between devices  816 us (52%)
  Pallas kernels  331 us (21%)
  starting transfers between devices  107 us (7%)
  blocking collectives  104 us (7%)
  other arithmetic  91.9 us (6%)
  local copies, waits for them, and re-layouts  75.1 us (5%)
  between operations  17.1 us (1%)
    all_gather x6, waiting for transfers between devices, gather(): return lax.all_gather(w, 'fsdp', axis=0, tiled=True)  234 us
    ppermute x8, waiting for transfers between devices, line_sum(): out = lax.ppermute(full, 'ctx', [(1, 0), (2, 3)])  197 us
    ppermute x27, waiting for transfers between devices, swap(): return lax.ppermute(v, axis, [(i, i ^ bit) for i in range(n)])  186 us
    all_gather x2, waiting for transfers between devices, per_device(): kvs.append(lax.all_gather(kv, 'ctx', axis=0, tiled=True))  113 us
    psum x1, blocking collectives, per_device(): gg = lax.psum(gg, ('fsdp', 'ctx'))  97.8 us
    pallas_call x7, Pallas kernels, weight_grad(): pl.pallas_call(functools.partial(wgrad_kernel, k), grid_spec=pltpu.Prefet...  91.8 us
    ppermute x8, waiting for transfers between devices, line_sum(): v = v + lax.ppermute(v, 'ctx', [(0, 1), (3, 2)])  84.7 us
    ppermute x8, starting transfers between devices, line_sum(): v = v + lax.ppermute(v, 'ctx', [(0, 1), (3, 2)])  60.4 us
  transfers between devices with their start and end apart: 69, of which 28 were waited for; matrix products, arithmetic and copies ran while one was open for 10% of the time, Pallas kernels for 15%

profile of v1, /device:TPU:0, one launch (start us, length us, event | category | flops | bytes accessed | tf_op | source)
XLA Modules:
  0.0 1548.8 jit_solution(1589464874031812672)
XLA Ops:
  24.3 39.4 %all-gather.9.cloned.1.call-done.w_ref = bf16[1536,2304]{1,0:T(8,128)(2,1)} async-done(((bf16[384,2304]{1,0:T(8,128)(2,1)}), bf16[1536,2304]{1,0:T(8,128)(2,1)}) %all-gather.9.cloned.1.call-update) | async-done | bytes 7077904 | tf_op jit(solution)/shard_map/all_gather | solution.py:726
  90.0 26.7 %all-gather.13.cloned.1.call-done = bf16[1536,2304]{1,0:T(8,128)(2,1)} async-done(((bf16[384,2304]{1,0:T(8,128)(2,1)}), bf16[1536,2304]{1,0:T(8,128)(2,1)}) %all-gather.13.cloned.1.call-update) | async-done | bytes 7077904 | tf_op jit(solution)/shard_map/all_gather | solution.py:726
  122.9 62.7 %all-gather.17.cloned.1.call-done.k_ref.v_ref = bf16[1088,1536]{1,0:T(8,128)(2,1)} async-done(((bf16[272,1536]{1,0:T(8,128)(2,1)}), bf16[1088,1536]{1,0:T(8,128)(2,1)}) %all-gather.17.cloned.1.call-update) | async-done | bytes 3342352 | tf_op jit(solution)/shard_map/all_gather | solution.py:756
  185.6 15.4 attention.3
  202.5 50.4 %all-gather.11.cloned.1.call-done.k_ref.v_ref = bf16[1088,1536]{1,0:T(8,128)(2,1)} async-done(((bf16[272,1536]{1,0:T(8,128)(2,1)}), bf16[1088,1536]{1,0:T(8,128)(2,1)}) %all-gather.11.cloned.1.call-update) | async-done | bytes 3342352 | tf_op jit(solution)/shard_map/all_gather | solution.py:756
  252.9 15.3 attention.2
  314.5 29.3 %all-gather.23.cloned.1.call-done.refs_10_ = bf16[1536,3072]{1,0:T(8,128)(2,1)} async-done(((bf16[384,3072]{1,0:T(8,128)(2,1)}), bf16[1536,3072]{1,0:T(8,128)(2,1)}) %all-gather.23.cloned.1.call-update) | async-done | bytes 9437200 | tf_op jit(solution)/shard_map/all_gather | solution.py:726
  343.8 65.8 %all-gather.19.cloned.1.call-done.refs_8_ = bf16[1536,3072]{1,0:T(8,128)(2,1)} async-done(((bf16[384,3072]{1,0:T(8,128)(2,1)}), bf16[1536,3072]{1,0:T(8,128)(2,1)}) %all-gather.19.cloned.1.call-update) | async-done | bytes 9437200 | tf_op jit(solution)/shard_map/all_gather | solution.py:726
  409.6 65.8 %all-gather.21.cloned.1.call-done.refs_9_ = bf16[1536,3072]{1,0:T(8,128)(2,1)} async-done(((bf16[384,3072]{1,0:T(8,128)(2,1)}), bf16[1536,3072]{1,0:T(8,128)(2,1)}) %all-gather.21.cloned.1.call-update) | async-done | bytes 9437200 | tf_op jit(solution)/shard_map/all_gather | solution.py:726
  476.3 53.0 %mlp.1 = (f32[544,1536]{1,0:T(8,128)}, bf16[544,1536]{1,0:T(8,128)(2,1)}, bf16[544,3072]{1,0:T(8,128)(2,1)}, bf16[544,3072]{1,0:T(8,128)(2,1)}, bf16[544,3072]{1...) custom-call(f32[272,1536]{1,0:T(8,128)} %get-tuple-element.82.refs_0_.x1_ref, ...), custom_call_target="tpu_custom_call" | custom-call | flops 30802968576 | bytes 55050240 | tf_op jit(solution)/shard_map/mlp/pallas_call | solution.py:328
  532.4 19.3 %collective-permute-done.5.b_ref = bf16[272,1536]{1,0:T(8,128)(2,1)S(1)} collective-permute-done((bf16[272,1536]{1,0:T(8,128)(2,1)S(1)}, bf16[272,1536]{1,0:T(8,128)(2,1)S(1)}, u32[]{:S(2)}, u32[]{:S(2)}) %collective-permute-start.5) | collective-permute-done | bytes 835616 | tf_op jit(solution)/shard_map/ppermute | solution.py:652
  552.6 16.2 %cross_back.2 = (f32[272,1536]{1,0:T(8,128)}, bf16[272,1536]{1,0:T(8,128)(2,1)}, f32[1,1536]{1,0:T(1,128)}, bf16[272,768]{1,0:T(8,128)(2,1)}, bf16[130,768]{1,0:...) custom-call(f32[544,1536]{1,0:T(8,128)} %get-tuple-element.89.x2_ref, bf16[544,1536]{1,0:T(8,128)(2,1)} %bitcast.47, ...), custom_call_target="tpu_custom_call" | custom-call | flops 1826586624 | bytes 13074432 | tf_op jit(solution)/shard_map/cross_back/pallas_call | solution.py:414
  570.3 18.6 %collective-permute-done.6.b_ref = bf16[272,1536]{1,0:T(8,128)(2,1)S(1)} collective-permute-done((bf16[272,1536]{1,0:T(8,128)(2,1)}, bf16[272,1536]{1,0:T(8,128)(2,1)S(1)}, u32[]{:S(2)}, u32[]{:S(2)}) %collective-permute-start.6) | collective-permute-done | bytes 835616 | tf_op jit(solution)/shard_map/ppermute | solution.py:652
  589.9 24.4 %attention_back.2 = (f32[272,1536]{1,0:T(8,128)}, bf16[272,1536]{1,0:T(8,128)(2,1)}, f32[1,1536]{1,0:T(1,128)}, bf16[272,768]{1,0:T(8,128)(2,1)}, bf16[1088,768]{1,0:T(8,128)(2,1)}, /*index=5*/bf16[1088,768]{1,0:T(8,128)(2,1)}) custom-call(f32[272,1536]{1,0:T(8,128)} %get-tuple-element.82.refs_0_.x1_ref, f32[272,1536]{1,0:T(8,128)} %get-tuple-element.93.g2x_ref, ...), custom_call_target="tpu_custom_call" | custom-call | flops 9732882432 | bytes 15728640 | tf_op jit(solution)/shard_map/attention_back/pallas_call | solution.py:495
  622.3 18.8 %weight_grad.13 = bf16[1536,3072]{1,0:T(8,128)(2,1)} custom-call(s32[4]{0:T(128)} %broadcast_xor_fusion.order_ref, bf16[544,1536]{1,0:T(8,128)(2,1)} %bitcast.48, bf16[544,3072]{1,0:T(8,128)(2,1)} %get-tuple-element.141.refs_1_), custom_call_target="tpu_custom_call" | custom-call | flops 5133828096 | bytes 19464192 | tf_op jit(solution)/shard_map/weight_grad/pallas_call | solution.py:628
  646.5 18.5 %weight_grad.12 = bf16[1536,3072]{1,0:T(8,128)(2,1)} custom-call(s32[4]{0:T(128)} %broadcast_xor_fusion.order_ref, bf16[544,1536]{1,0:T(8,128)(2,1)} %get-tuple-element.138.refs_0_, bf16[544,3072]{1,0:T(8,128)(2,1)} %get-tuple-element.140.refs_1_), custom_call_target="tpu_custom_call" | custom-call | flops 5133828096 | bytes 19464192 | tf_op jit(solution)/shard_map/weight_grad/pallas_call | solution.py:628
  670.1 18.5 %weight_grad.11 = bf16[1536,3072]{1,0:T(8,128)(2,1)} custom-call(s32[4]{0:T(128)} %broadcast_xor_fusion.order_ref, bf16[544,1536]{1,0:T(8,128)(2,1)} %get-tuple-element.138.refs_0_, bf16[544,3072]{1,0:T(8,128)(2,1)} %get-tuple-element.139.refs_1_), custom_call_target="tpu_custom_call" | custom-call | flops 5133828096 | bytes 19464192 | tf_op jit(solution)/shard_map/weight_grad/pallas_call | solution.py:628
  694.4 16.2 %cross_back.3 = (f32[272,1536]{1,0:T(8,128)}, bf16[272,1536]{1,0:T(8,128)(2,1)}, f32[1,1536]{1,0:T(1,128)}, bf16[272,768]{1,0:T(8,128)(2,1)}, bf16[130,768]{1,0:...) custom-call(f32[544,1536]{1,0:T(8,128)} %get-tuple-element.89.x2_ref, bf16[544,1536]{1,0:T(8,128)(2,1)} %bitcast.49, ...), custom_call_target="tpu_custom_call" | custom-call | flops 1826586624 | bytes 13074432 | tf_op jit(solution)/shard_map/cross_back/pallas_call | solution.py:414
  738.0 16.1 %collective-permute-done.9.b_ref = bf16[272,1536]{1,0:T(8,128)(2,1)} collective-permute-done((bf16[272,1536]{1,0:T(8,128)(2,1)}, bf16[272,1536]{1,0:T(8,128)(2,1)}, u32[]{:S(2)}, u32[]{:S(2)}) %collective-permute-start.9) | collective-permute-done | bytes 835616 | tf_op jit(solution)/shard_map/ppermute | solution.py:652
  754.0 24.6 %attention_back.3 = (f32[272,1536]{1,0:T(8,128)}, bf16[272,1536]{1,0:T(8,128)(2,1)}, f32[1,1536]{1,0:T(1,128)}, bf16[272,768]{1,0:T(8,128)(2,1)}, bf16[1088,768]{1,0:T(8,128)(2,1)}, /*index=5*/bf16[1088,768]{1,0:T(8,128)(2,1)}) custom-call(f32[272,1536]{1,0:T(8,128)} %get-tuple-element.86.refs_1_.x1_ref, f32[272,1536]{1,0:T(8,128)} %get-tuple-element.103.g2x_ref, ...), custom_call_target="tpu_custom_call" | custom-call | flops 9732882432 | bytes 15728640 | tf_op jit(solution)/shard_map/attention_back/pallas_call | solution.py:495
  854.0 23.4 %collective-permute-done.37 = bf16[384,768]{1,0:T(8,128)(2,1)S(1)} collective-permute-done((bf16[384,768]{1,0:T(8,128)(2,1)S(1)}, bf16[384,768]{1,0:T(8,128)(2,1)S(1)}, u32[]{:S(2)}, u32[]{:S(2)}) %collective-permute-start.37) | collective-permute-done | bytes 589856 | tf_op jit(solution)/shard_map/ppermute | solution.py:677
  893.0 26.0 %collective-permute-start.19 = (bf16[384,768]{1,0:T(8,128)(2,1)S(1)}, bf16[384,768]{1,0:T(8,128)(2,1)S(1)}, u32[]{:S(2)}, u32[]{:S(2)}) collective-permute-start(bf16[384,768]{1,0:T(8,128)(2,1)S(1)} %slice_add_fusion.15), channel_id=1, source_target_pairs={{0,2},{6,4},{1,3},{7,5},{8,10},{14,12},{9,11},{15,13},{16,18},{22,... | collective-permute-start | bytes 1769480 | tf_op jit(solution)/shard_map/ppermute | solution.py:677
  991.1 34.8 %collective-permute-done.54 = bf16[384,3072]{1,0:T(8,128)(2,1)} collective-permute-done((bf16[384,3072]{1,0:T(8,128)(2,1)}, bf16[384,3072]{1,0:T(8,128)(2,1)}, u32[]{:S(2)}, u32[]{:S(2)}) %collective-permute-start.54) | collective-permute-done | bytes 2359328 | tf_op jit(solution)/shard_map/ppermute | solution.py:652
  1056.8 15.7 %weight_grad.7 = bf16[1536,2304]{1,0:T(8,128)(2,1)} custom-call(s32[4]{0:T(128)} %broadcast_xor_fusion.order_ref, bf16[272,1536]{1,0:T(8,128)(2,1)} %get-tuple-element.118.refs_0_, bf16[272,1536]{1,0:T(8,128)(2,1)} %get-tuple-element.119.refs_1_, bf16[272,2304]{1,0:T(8,128)(2,1)} %get-tuple-element.120.refs_2_, bf16[272,2304]{1,0:T(8,128)(2,1)} %get-tuple-element.121.refs_3_), custom_call_target="tpu_custom_call" | custom-call | flops 3850371072 | bytes 14598144 | tf_op jit(solution)/shard_map/weight_grad/pallas_call | solution.py:628
  1087.2 29.9 %collective-permute-done.42 = bf16[384,3072]{1,0:T(8,128)(2,1)} collective-permute-done((bf16[384,3072]{1,0:T(8,128)(2,1)}, bf16[384,3072]{1,0:T(8,128)(2,1)}, u32[]{:S(2)}, u32[]{:S(2)}) %collective-permute-start.42) | collective-permute-done | bytes 2359328 | tf_op jit(solution)/shard_map/ppermute | solution.py:652
  1144.0 97.8 %psum.7 = f32[3,1536]{1,0:T(4,128)S(1)} all-reduce(f32[3,1536]{1,0:T(4,128)S(1)} %pad_maximum_fusion.14), channel_id=1, replica_groups=mesh['fsdp'=4,'ctx'=4,'tp'=2] {'fsdp','ctx'}, use_global_device_ids=true, to_apply=%region_2.3 | all-reduce | flops 4608 | bytes 36864 | tf_op jit(solution)/shard_map/psum | solution.py:840
  1263.0 33.4 %collective-permute-done.12 = bf16[384,2304]{1,0:T(8,128)(2,1)S(1)} collective-permute-done((bf16[384,2304]{1,0:T(8,128)(2,1)S(1)}, bf16[384,2304]{1,0:T(8,128)(2,1)S(1)}, u32[]{:S(2)}, u32[]{:S(2)}) %collective-permute-start.12) | collective-permute-done | bytes 1769504 | tf_op jit(solution)/shard_map/ppermute | solution.py:652
  1310.7 28.0 %collective-permute-done.13 = bf16[384,2304]{1,0:T(8,128)(2,1)S(1)} collective-permute-done((bf16[384,2304]{1,0:T(8,128)(2,1)S(1)}, bf16[384,2304]{1,0:T(8,128)(2,1)S(1)}, u32[]{:S(2)}, u32[]{:S(2)}) %collective-permute-start.13) | collective-permute-done | bytes 1769504 | tf_op jit(solution)/shard_map/ppermute | solution.py:677
  1350.4 55.8 %collective-permute-done.58 = bf16[384,3072]{1,0:T(8,128)(2,1)S(1)} collective-permute-done((bf16[384,3072]{1,0:T(8,128)(2,1)S(1)}, bf16[384,3072]{1,0:T(8,128)(2,1)S(1)}, u32[]{:S(2)}, u32[]{:S(2)}) %collective-permute-start.58) | collective-permute-done | bytes 2359328 | tf_op jit(solution)/shard_map/ppermute | solution.py:683
  1415.2 41.6 %collective-permute-done.52 = bf16[384,3072]{1,0:T(8,128)(2,1)} collective-permute-done((bf16[384,3072]{1,0:T(8,128)(2,1)}, bf16[384,3072]{1,0:T(8,128)(2,1)}, u32[]{:S(2)}, u32[]{:S(2)}) %collective-permute-start.52) | collective-permute-done | bytes 2359328 | tf_op jit(solution)/shard_map/ppermute | solution.py:683
  1461.5 45.9 %collective-permute-done.46 = bf16[384,3072]{1,0:T(8,128)(2,1)} collective-permute-done((bf16[384,3072]{1,0:T(8,128)(2,1)}, bf16[384,3072]{1,0:T(8,128)(2,1)}, u32[]{:S(2)}, u32[]{:S(2)}) %collective-permute-start.46) | collective-permute-done | bytes 2359328 | tf_op jit(solution)/shard_map/ppermute | solution.py:683
  1512.1 25.7 %collective-permute-done.16 = bf16[384,2304]{1,0:T(8,128)(2,1)} collective-permute-done((bf16[384,2304]{1,0:T(8,128)(2,1)}, bf16[384,2304]{1,0:T(8,128)(2,1)}, u32[]{:S(2)}, u32[]{:S(2)}) %collective-permute-start.16) | collective-permute-done | bytes 1769504 | tf_op jit(solution)/shard_map/ppermute | solution.py:683
  (403 shorter events, 458.6 us)
Async XLA Ops:
  7.2 56.5 %all-gather.9.cloned.1.call-start = ((), (), s32[]{:S(2)}) async-start(), calls=%async_computation.2 | async-start | bytes 8847360 | tf_op jit(solution)/shard_map/all_gather | solution.py:726
  10.0 106.7 %all-gather.13.cloned.1.call-start = ((), (), s32[]{:S(2)}) async-start(), calls=%async_computation.4 | async-start | bytes 8847360 | tf_op jit(solution)/shard_map/all_gather | solution.py:726
  13.0 172.6 %all-gather.17.cloned.1.call-start = ((), (), s32[]{:S(2)}) async-start(), calls=%async_computation.6 | async-start | bytes 4177920 | tf_op jit(solution)/shard_map/all_gather | solution.py:756
  73.6 179.3 %all-gather.11.cloned.1.call-start = ((), (), s32[]{:S(2)}) async-start(), calls=%async_computation.3 | async-start | bytes 4177920 | tf_op jit(solution)/shard_map/all_gather | solution.py:756
  84.0 193.5 %all-gather.15.cloned.1.call-start = ((), (), s32[]{:S(2)}) async-start(), calls=%async_computation.5 | async-start | bytes 2949120 | tf_op jit(solution)/shard_map/all_gather | solution.py:726
  85.0 258.8 %all-gather.23.cloned.1.call-start = ((), (), s32[]{:S(2)}) async-start(), calls=%async_computation.9 | async-start | bytes 11796480 | tf_op jit(solution)/shard_map/all_gather | solution.py:726
  88.5 321.1 %all-gather.19.cloned.1.call-start = ((), (), s32[]{:S(2)}) async-start(), calls=%async_computation.7 | async-start | bytes 11796480 | tf_op jit(solution)/shard_map/all_gather | solution.py:726
  89.3 386.2 %all-gather.21.cloned.1.call-start = ((), (), s32[]{:S(2)}) async-start(), calls=%async_computation.8 | async-start | bytes 11796480 | tf_op jit(solution)/shard_map/all_gather | solution.py:726
  90.0 943.2 %reduce-scatter.3.cloned.1.call-start = ((), (), s32[]{:S(2)}) async-start(), calls=%async_computation.10 | async-start | bytes 4177920 | tf_op jit(solution)/shard_map/reduce_scatter | solution.py:810
  201.0 80.9 %collective-permute-start.1 = (bf16[272,1536]{1,0:T(8,128)(2,1)}, bf16[272,1536]{1,0:T(8,128)(2,1)S(1)}, u32[]{:S(2)}, u32[]{:S(2)}) collective-permute-start(bf16[272,1536]{1,0:T(8,128)(2,1)} %get-tuple-element.85.a_ref), channel_id=1, source_target_pairs={{0,1},{1,0},{2,3},{3,2},{4,5},{5,4},{6,7},{7,6},{8,9},{9,8},{10,11... | collective-permute-start | bytes 2506760 | tf_op jit(solution)/shard_map/ppermute | solution.py:652
  295.4 180.1 %collective-permute-start.3 = (bf16[272,1536]{1,0:T(8,128)(2,1)}, bf16[272,1536]{1,0:T(8,128)(2,1)}, u32[]{:S(2)}, u32[]{:S(2)}) collective-permute-start(bf16[272,1536]{1,0:T(8,128)(2,1)} %get-tuple-element.88.refs_3_), channel_id=1, source_target_pairs={{0,1},{1,0},{2,3},{3,2},{4,5},{5,4},{6,7},{7,6},{8,9},{9,8},{10,11... | collective-permute-start | bytes 2506760 | tf_op jit(solution)/shard_map/ppermute | solution.py:652
  310.4 165.0 %collective-permute-start.2 = (bf16[272,1536]{1,0:T(8,128)(2,1)}, bf16[272,1536]{1,0:T(8,128)(2,1)S(1)}, u32[]{:S(2)}, u32[]{:S(2)}) collective-permute-start(bf16[272,1536]{1,0:T(8,128)(2,1)} %get-tuple-element.87.refs_2_), channel_id=1, source_target_pairs={{0,1},{1,0},{2,3},{3,2},{4,5},{5,4},{6,7},{7,6},{8,9},{9,8},{10,11... | collective-permute-start | bytes 2506760 | tf_op jit(solution)/shard_map/ppermute | solution.py:652
  618.3 426.7 %reduce-scatter.5.cloned.1.call-start = ((), (), s32[]{:S(2)}) async-start(), calls=%async_computation.11 | async-start | bytes 4177920 | tf_op jit(solution)/shard_map/reduce_scatter | solution.py:810
  620.8 112.1 %collective-permute-start.4 = (bf16[544,1536]{1,0:T(8,128)(2,1)}, bf16[544,1536]{1,0:T(8,128)(2,1)}, u32[]{:S(2)}, u32[]{:S(2)}) collective-permute-start(bf16[544,1536]{1,0:T(8,128)(2,1)} %get-tuple-element.90), channel_id=1, source_target_pairs={{0,1},{1,0},{2,3},{3,2},{4,5},{5,4},{6,7},{7,6},{8,9},{9,8},{10,11... | collective-permute-start | bytes 5013512 | tf_op jit(solution)/shard_map/ppermute | solution.py:652
  646.0 321.0 %collective-permute-start.53 = (bf16[768,3072]{1,0:T(8,128)(2,1)}, bf16[768,3072]{1,0:T(8,128)(2,1)}, u32[]{:S(2)}, u32[]{:S(2)}) collective-permute-start(bf16[768,3072]{1,0:T(8,128)(2,1)} %slice.349), channel_id=1, source_target_pairs={{0,8},{8,0},{16,24},{24,16},{1,9},{9,1},{17,25},{25,17},{2,10},{10... | collective-permute-start | bytes 14155784 | tf_op jit(solution)/shard_map/ppermute | solution.py:652
  669.9 305.9 %collective-permute-start.47 = (bf16[768,3072]{1,0:T(8,128)(2,1)}, bf16[768,3072]{1,0:T(8,128)(2,1)}, u32[]{:S(2)}, u32[]{:S(2)}) collective-permute-start(bf16[768,3072]{1,0:T(8,128)(2,1)} %slice.343), channel_id=1, source_target_pairs={{0,8},{8,0},{16,24},{24,16},{1,9},{9,1},{17,25},{25,17},{2,10},{10... | collective-permute-start | bytes 14155784 | tf_op jit(solution)/shard_map/ppermute | solution.py:652
  719.8 74.9 %collective-permute-start.35 = (bf16[768,768]{1,0:T(8,128)(2,1)}, bf16[768,768]{1,0:T(8,128)(2,1)}, u32[]{:S(2)}, u32[]{:S(2)}) collective-permute-start(bf16[768,768]{1,0:T(8,128)(2,1)} %slice.331), channel_id=1, source_target_pairs={{0,8},{8,0},{16,24},{24,16},{1,9},{9,1},{17,25},{25,17},{2,10},{10... | collective-permute-start | bytes 3538952 | tf_op jit(solution)/shard_map/ppermute | solution.py:652
  722.8 69.6 %collective-permute-start.29 = (bf16[384,1536]{1,0:T(8,128)(2,1)}, bf16[384,1536]{1,0:T(8,128)(2,1)}, u32[]{:S(2)}, u32[]{:S(2)}) collective-permute-start(bf16[384,1536]{1,0:T(8,128)(2,1)} %slice.323), channel_id=1, source_target_pairs={{0,8},{8,0},{16,24},{24,16},{1,9},{9,1},{17,25},{25,17},{2,10},{10... | collective-permute-start | bytes 3538952 | tf_op jit(solution)/shard_map/ppermute | solution.py:652
  877.4 106.4 %collective-permute-start.41 = (bf16[768,3072]{1,0:T(8,128)(2,1)}, bf16[768,3072]{1,0:T(8,128)(2,1)}, u32[]{:S(2)}, u32[]{:S(2)}) collective-permute-start(bf16[768,3072]{1,0:T(8,128)(2,1)} %slice.337), channel_id=1, source_target_pairs={{0,8},{8,0},{16,24},{24,16},{1,9},{9,1},{17,25},{25,17},{2,10},{10... | collective-permute-start | bytes 14155784 | tf_op jit(solution)/shard_map/ppermute | solution.py:652
  948.0 132.6 %collective-permute-start.28 = (bf16[384,768]{1,0:T(8,128)(2,1)}, bf16[384,768]{1,0:T(8,128)(2,1)}, u32[]{:S(2)}, u32[]{:S(2)}) collective-permute-start(bf16[384,768]{1,0:T(8,128)(2,1)} %pad_maximum_fusion.11), channel_id=1, source_target_pairs={{2,0},{4,6},{3,1},{5,7},{10,8},{12,14},{11,9},{13,15},{18,16},{20,... | collective-permute-start | bytes 1769480 | tf_op jit(solution)/shard_map/ppermute | solution.py:683
  973.8 111.9 %collective-permute-start.22 = (bf16[384,768]{1,0:T(8,128)(2,1)}, bf16[384,768]{1,0:T(8,128)(2,1)}, u32[]{:S(2)}, u32[]{:S(2)}) collective-permute-start(bf16[384,768]{1,0:T(8,128)(2,1)} %pad_maximum_fusion.10), channel_id=1, source_target_pairs={{2,0},{4,6},{3,1},{5,7},{10,8},{12,14},{11,9},{13,15},{18,16},{20,... | collective-permute-start | bytes 1769480 | tf_op jit(solution)/shard_map/ppermute | solution.py:683
  983.2 93.3 %collective-permute-start.48 = (bf16[384,3072]{1,0:T(8,128)(2,1)}, bf16[384,3072]{1,0:T(8,128)(2,1)}, u32[]{:S(2)}, u32[]{:S(2)}) collective-permute-start(bf16[384,3072]{1,0:T(8,128)(2,1)} %slice.345), channel_id=1, source_target_pairs={{0,16},{8,24},{16,0},{24,8},{1,17},{9,25},{17,1},{25,9},{2,18},{10... | collective-permute-start | bytes 7077896 | tf_op jit(solution)/shard_map/ppermute | solution.py:652
  989.7 127.5 %collective-permute-start.42 = (bf16[384,3072]{1,0:T(8,128)(2,1)}, bf16[384,3072]{1,0:T(8,128)(2,1)}, u32[]{:S(2)}, u32[]{:S(2)}) collective-permute-start(bf16[384,3072]{1,0:T(8,128)(2,1)} %slice.339), channel_id=1, source_target_pairs={{0,16},{8,24},{16,0},{24,8},{1,17},{9,25},{17,1},{25,9},{2,18},{10... | collective-permute-start | bytes 7077896 | tf_op jit(solution)/shard_map/ppermute | solution.py:652
  1027.9 217.1 %collective-permute-start.55 = (bf16[384,3072]{1,0:T(8,128)(2,1)S(1)}, bf16[384,3072]{1,0:T(8,128)(2,1)}, u32[]{:S(2)}, u32[]{:S(2)}) collective-permute-start(bf16[384,3072]{1,0:T(8,128)(2,1)S(1)} %slice_add_fusion.4), channel_id=1, source_target_pairs={{0,2},{6,4},{1,3},{7,5},{8,10},{14,12},{9,11},{15,13},{16,18},{22,... | collective-permute-start | bytes 7077896 | tf_op jit(solution)/shard_map/ppermute | solution.py:677
  1076.5 179.8 %collective-permute-start.11 = (bf16[768,2304]{1,0:T(8,128)(2,1)}, bf16[768,2304]{1,0:T(8,128)(2,1)}, u32[]{:S(2)}, u32[]{:S(2)}) collective-permute-start(bf16[768,2304]{1,0:T(8,128)(2,1)} %slice.302), channel_id=1, source_target_pairs={{0,8},{8,0},{16,24},{24,16},{1,9},{9,1},{17,25},{25,17},{2,10},{10... | collective-permute-start | bytes 10616840 | tf_op jit(solution)/shard_map/ppermute | solution.py:652
  1080.6 167.9 %collective-permute-start.49 = (bf16[384,3072]{1,0:T(8,128)(2,1)}, bf16[384,3072]{1,0:T(8,128)(2,1)}, u32[]{:S(2)}, u32[]{:S(2)}) collective-permute-start(bf16[384,3072]{1,0:T(8,128)(2,1)} %slice_add_fusion.5), channel_id=1, source_target_pairs={{0,2},{6,4},{1,3},{7,5},{8,10},{14,12},{9,11},{15,13},{16,18},{22,... | collective-permute-start | bytes 7077896 | tf_op jit(solution)/shard_map/ppermute | solution.py:677
  1123.5 129.5 %collective-permute-start.43 = (bf16[384,3072]{1,0:T(8,128)(2,1)}, bf16[384,3072]{1,0:T(8,128)(2,1)}, u32[]{:S(2)}, u32[]{:S(2)}) collective-permute-start(bf16[384,3072]{1,0:T(8,128)(2,1)} %slice_add_fusion.6), channel_id=1, source_target_pairs={{0,2},{6,4},{1,3},{7,5},{8,10},{14,12},{9,11},{15,13},{16,18},{22,... | collective-permute-start | bytes 7077896 | tf_op jit(solution)/shard_map/ppermute | solution.py:677
  1262.2 77.7 %collective-permute-start.51 = (bf16[192,3072]{1,0:T(8,128)(2,1)S(1)}, bf16[192,3072]{1,0:T(8,128)(2,1)S(1)}, u32[]{:S(2)}, u32[]{:S(2)}) collective-permute-start(bf16[192,3072]{1,0:T(8,128)(2,1)S(1)} %select_add_fusion.1), channel_id=1, source_target_pairs={{2,4},{4,2},{3,5},{5,3},{10,12},{12,10},{11,13},{13,11},{18,20},{2... | collective-permute-start | bytes 3538952 | tf_op jit(solution)/shard_map/ppermute | solution.py:681
  1309.4 96.8 %collective-permute-start.58 = (bf16[384,3072]{1,0:T(8,128)(2,1)S(1)}, bf16[384,3072]{1,0:T(8,128)(2,1)S(1)}, u32[]{:S(2)}, u32[]{:S(2)}) collective-permute-start(bf16[384,3072]{1,0:T(8,128)(2,1)S(1)} %pad_maximum_fusion.4), channel_id=1, source_target_pairs={{2,0},{4,6},{3,1},{5,7},{10,8},{12,14},{11,9},{13,15},{18,16},{20,... | collective-permute-start | bytes 7077896 | tf_op jit(solution)/shard_map/ppermute | solution.py:683
  1341.7 115.1 %collective-permute-start.52 = (bf16[384,3072]{1,0:T(8,128)(2,1)}, bf16[384,3072]{1,0:T(8,128)(2,1)}, u32[]{:S(2)}, u32[]{:S(2)}) collective-permute-start(bf16[384,3072]{1,0:T(8,128)(2,1)} %pad_maximum_fusion.3), channel_id=1, source_target_pairs={{2,0},{4,6},{3,1},{5,7},{10,8},{12,14},{11,9},{13,15},{18,16},{20,... | collective-permute-start | bytes 7077896 | tf_op jit(solution)/shard_map/ppermute | solution.py:683
  1345.9 161.6 %collective-permute-start.46 = (bf16[384,3072]{1,0:T(8,128)(2,1)}, bf16[384,3072]{1,0:T(8,128)(2,1)}, u32[]{:S(2)}, u32[]{:S(2)}) collective-permute-start(bf16[384,3072]{1,0:T(8,128)(2,1)} %pad_maximum_fusion.2), channel_id=1, source_target_pairs={{2,0},{4,6},{3,1},{5,7},{10,8},{12,14},{11,9},{13,15},{18,16},{20,... | collective-permute-start | bytes 7077896 | tf_op jit(solution)/shard_map/ppermute | solution.py:683
  1349.1 188.8 %collective-permute-start.16 = (bf16[384,2304]{1,0:T(8,128)(2,1)}, bf16[384,2304]{1,0:T(8,128)(2,1)}, u32[]{:S(2)}, u32[]{:S(2)}) collective-permute-start(bf16[384,2304]{1,0:T(8,128)(2,1)} %pad_maximum_fusion.7), channel_id=1, source_target_pairs={{2,0},{4,6},{3,1},{5,7},{10,8},{12,14},{11,9},{13,15},{18,16},{20,... | collective-permute-start | bytes 5308424 | tf_op jit(solution)/shard_map/ppermute | solution.py:683
  (103 other events, 1890.1 us)
Sparse Core Ops, SparseCore 0:
  10.1 53.5 all-gather.8
  65.8 50.8 all-gather.12
  118.8 66.6 all-gather.16
  187.6 65.2 all-gather.10
  254.9 22.6 all-gather.14
  279.6 64.2 all-gather.22
  345.4 64.2 all-gather.18
  411.2 64.2 all-gather.20
  618.4 63.4 reduce-scatter.2
  791.7 87.0 reduce-scatter.4
